TPU v7x, 32 devices: a whole 2x2x4 slice. The times are simulated.
32 devices in a mesh: wide: 8 (over y, x, core), narrow: 4 (over z).
Axes of the slice: x: 2, y: 2, z: 4, core: 2. Of those that a mesh axis runs over, the one named last changes fastest.
Arguments:
- activity: bfloat16 [32, 8, 512, 512], P(('wide', 'narrow')), may hold values from 0 to 1
- tile_coords: int32 [32, 2], replicated, may hold values from 0 to 7, as said below
- user_owner: int32 [8], replicated, may hold values from 0 to 7, each once
- item_owner: int32 [8], replicated, may hold values from 0 to 7, each once
- user_factor: float32 [4096, 256], P('wide', 'narrow'), may hold values from 0 to 1
- item_factor: float32 [4096, 256], P('wide', 'narrow'), may hold values from 0 to 1
- time_factor: float32 [8, 256], replicated, may hold values from 0.0003 to 0.003
- user_dual: float32 [4096, 256], P('wide', 'narrow'), may hold values from -1.8 to 1.8
- item_dual: float32 [4096, 256], P('wide', 'narrow'), may hold values from -1.8 to 1.8
Outputs:
- new_users: float32 [4096, 256], P('wide', 'narrow')
- new_items: float32 [4096, 256], P('wide', 'narrow')
- new_user_dual: float32 [4096, 256], P('wide', 'narrow')
- new_item_dual: float32 [4096, 256], P('wide', 'narrow')
Inputs may be any that keep to these rules, and one draw needn't show every extreme that they name: `tile_coords`: no pair of blocks appears twice. `user_owner`: each stored row block holds exactly one user block. `item_owner`: each stored row block holds exactly one item block.
All inputs are finite; a program needn't handle non-finite values.
Results may differ from a plain program's by a relative error of at most 0.0017.
The roundings to bfloat16 on the way count: a program that leaves them out, or rounds other values in their place, can miss the bound.
Values may be sent and summed in bfloat16 or wider, within the bound.
No kernel may reach another device: no remote copies, remote signals or barrier semaphores. Data moves between devices by JAX's collectives and lax.ppermute only.
A program may use at most 64 MiB of HBM per device.

v0:
```python
import functools

import jax
import jax.numpy as jnp
from jax import lax
from jax.experimental import pallas as pl
from jax.experimental.pallas import tpu as pltpu
from jax.sharding import PartitionSpec as P


PASSES = 2
LEAF = 8
HIGHEST = lax.Precision.HIGHEST
ROOM = pltpu.CompilerParams(vmem_limit_bytes=16 * 2**20)


def eliminate(left, right):
    panel, width = left.shape
    lane = lax.broadcasted_iota(jnp.int32, (LEAF, width), 1)
    sub = lax.broadcasted_iota(jnp.int32, (LEAF, width), 0)
    for j in range(0, panel, LEAF):
        cols = [jnp.broadcast_to(left[:, j + m : j + m + 1], (panel, width)) for m in range(LEAF)]
        d = [c[j : j + LEAF] for c in cols]
        for k in range(LEAF):
            r = 1.0 / d[k][k : k + 1]
            pivot = d[k]
            here = sub == k
            for m in range(LEAF):
                if m != k:
                    f = d[m][k : k + 1] * r
                    d[m] = jnp.where(here, f, d[m] - pivot * f)
            d[k] = jnp.where(here, r, -pivot * r)
        inside = (lane >= j) & (lane < j + LEAF)
        el = jnp.where(inside, jnp.where(lane == sub + j, 1.0, 0.0), left[j : j + LEAF])
        er = right[j : j + LEAF]
        rl = sum(d[m] * el[m : m + 1] for m in range(LEAF))
        rr = sum(d[m] * er[m : m + 1] for m in range(LEAF))
        new_left, new_right = [], []
        for i in range(0, panel, LEAF):
            if i == j:
                new_left.append(rl)
                new_right.append(rr)
            else:
                c = [col[i : i + LEAF] for col in cols]
                ul = sum(c[m] * rl[m : m + 1] for m in range(LEAF))
                ur = sum(c[m] * rr[m : m + 1] for m in range(LEAF))
                new_left.append(jnp.where(inside, 0.0, left[i : i + LEAF]) - ul)
                new_right.append(right[i : i + LEAF] - ur)
        left = jnp.concatenate(new_left, 0)
        right = jnp.concatenate(new_right, 0)
    return left, right


def eliminate_panel(panel, k, work_ref):
    rank = work_ref.shape[0]
    half = rank // 2
    lane = lax.broadcasted_iota(jnp.int32, (1, rank), 1)
    rows = pl.ds(k * panel, panel)
    left, right = eliminate(work_ref[rows, :half], work_ref[rows, half:])
    done = jnp.concatenate([left, right], 1)
    full = work_ref[...]
    change = jnp.dot(full[:, :panel], done, precision=HIGHEST, preferred_element_type=jnp.float32)
    work_ref[...] = pltpu.roll(jnp.where(lane < panel, 0.0, full) - change, rank - panel, 1)
    work_ref[rows, :] = pltpu.roll(done, rank - panel, 1)


def first_half_kernel(panel, time_ref, *refs):
    pieces, (work_ref, penalty_ref) = refs[:-2], refs[-2:]
    rank = work_ref.shape[0]
    height = pieces[0].shape[0]
    wide = lax.axis_index("wide")
    for r, piece in enumerate(pieces):
        place = wide ^ r
        start = (place % 2) * (rank // 2) + (place // 2) * height
        work_ref[pl.ds(pl.multiple_of(start, height), height), :] = piece[...]
    time = time_ref[...]
    times = lax.dot_general(
        time, time, (((0,), (0,)), ((), ())), precision=HIGHEST, preferred_element_type=jnp.float32
    )
    gram = work_ref[...] * times
    row = lax.broadcasted_iota(jnp.int32, (rank, rank), 0)
    col = lax.broadcasted_iota(jnp.int32, (rank, rank), 1)
    trace = jnp.sum(jnp.where(row == col, gram, 0.0), axis=0, keepdims=True)
    penalty = jnp.sum(trace, axis=1, keepdims=True) / rank
    penalty_ref[...] = jnp.broadcast_to(penalty, penalty_ref.shape)
    work_ref[...] = gram + jnp.where(row == col, penalty, 0.0)
    eliminate_panel(panel, 0, work_ref)


def second_half_kernel(panel, half_ref, inverse_ref):
    inverse_ref[...] = half_ref[...]
    eliminate_panel(panel, 1, inverse_ref)


def penalty_inverse(pieces, time_factor):
    rank = time_factor.shape[1]
    half, penalty = kernel_call(
        functools.partial(first_half_kernel, rank // 2),
        [shape((rank, rank)), shape((1, 128))], time_factor, *pieces, flops=6_000_000_000,
    )
    (inverse,) = kernel_call(
        functools.partial(second_half_kernel, rank // 2),
        [shape((rank, rank))], half, flops=6_000_000_000,
    )
    return penalty, inverse


def kernel_call(kernel, out_shape, *args, scratch=(), flops=1_000_000, smem=False):
    spec = pl.BlockSpec(memory_space=pltpu.SMEM) if smem else pl.BlockSpec(memory_space=pltpu.VMEM)
    size = sum(x.size * x.dtype.itemsize for x in (*args, *out_shape))
    return pl.pallas_call(
        kernel,
        out_shape=tuple(out_shape),
        in_specs=[spec] * len(args),
        out_specs=tuple(pl.BlockSpec(memory_space=pltpu.VMEM) for _ in out_shape),
        scratch_shapes=list(scratch),
        compiler_params=ROOM,
        cost_estimate=pl.CostEstimate(flops=flops, bytes_accessed=size, transcendentals=0),
    )(*args)


def shape(dims, dtype=jnp.float32):
    return jax.ShapeDtypeStruct(tuple(dims), dtype)


def swap(x, axis, mask):
    size = lax.axis_size(axis)
    return lax.ppermute(x, axis, [(i, i ^ mask) for i in range(size)])


def swaps(pieces):
    return [pieces[0]] + [swap(pieces[d], "narrow", d) for d in range(1, len(pieces))]


def for_each_position(body):
    me = lax.axis_index("narrow")
    for v in range(lax.axis_size("narrow")):
        pl.when(me == v)(functools.partial(body, v))


def rows_of(d, height):
    return pl.ds(pl.multiple_of((lax.axis_index("narrow") ^ d) * height, height), height)


def positions_kernel(coords_ref, user_ref, item_ref, table_ref):
    wide, narrow = lax.axis_index("wide"), lax.axis_index("narrow")
    count = lax.axis_size("narrow")
    for d in range(count):
        tile = wide * count + (narrow ^ d)
        user = user_ref[coords_ref[tile, 0]] ^ wide
        item = item_ref[coords_ref[tile, 1]] ^ wide
        table_ref[d : d + 1, :] = jnp.full((1, 128), user, jnp.int32)
        table_ref[count + d : count + d + 1, :] = jnp.full((1, 128), item, jnp.int32)


def positions(tile_coords, user_owner, item_owner):
    count = lax.axis_size("narrow")
    (table,) = kernel_call(
        positions_kernel, [shape((2 * count, 128), jnp.int32)],
        tile_coords, user_owner, item_owner, smem=True,
    )
    return table[:count], table[count:]


def start_kernel(factor_ref, low_ref, *outputs):
    low_ref[...] = factor_ref[...].astype(low_ref.dtype)
    split_kernel(len(outputs), factor_ref, *outputs)


def start(factor):
    count = lax.axis_size("narrow")
    height, rows = factor.shape
    out = [shape(factor.shape, jnp.bfloat16)] + [shape((height, rows // count))] * count
    low, *pieces = kernel_call(start_kernel, out, factor)
    return low, pieces


def split_kernel(count, *refs):
    inputs, outputs = refs[: -count], refs[-count:]
    width = outputs[0].shape[1]
    height = inputs[0].shape[0]

    def body(v):
        for d, out in enumerate(outputs):
            lanes = slice((v ^ d) * width, ((v ^ d) + 1) * width)
            first = inputs[0][:, lanes]
            if len(inputs) > 1:
                first = first + inputs[1][:, lanes]
            out[:height, :] = first
            for k in range(1, len(inputs)):
                out[k * height : (k + 1) * height, :] = inputs[k][:, lanes]

    for_each_position(body)


def split(*arrays):
    count = lax.axis_size("narrow")
    height, rows = arrays[0].shape
    out = [shape((len(arrays) * height, rows // count))] * count
    return kernel_call(functools.partial(split_kernel, count), out, *arrays)


def halves(gram, give_ref, keep_ref):
    half = keep_ref.shape[0]
    for core in range(2):

        @pl.when(lax.axis_index("wide") % 2 == core)
        def _(core=core):
            keep_ref[...] = gram[core * half : (core + 1) * half]
            give_ref[...] = gram[(1 - core) * half : (2 - core) * half]


def gram_of(rows):
    return lax.dot_general(
        rows, rows, (((1,), (1,)), ((), ())), precision=HIGHEST, preferred_element_type=jnp.float32
    )


def gram_kernel(*refs):
    pieces, (rows_ref, give_ref, keep_ref) = refs[:-3], refs[-3:]
    height = pieces[0].shape[0]
    for d, piece in enumerate(pieces):
        rows_ref[rows_of(d, height), :] = piece[...]
    halves(gram_of(rows_ref[...]), give_ref, keep_ref)


def assemble_kernel(*refs):
    factor_ref, pieces, outputs = refs[0], refs[1:-4], refs[-4:]
    height = pieces[0].shape[0] // 3
    for d, piece in enumerate(pieces):
        rows = rows_of(d, height)
        outputs[0][rows, :] = piece[:height]
        outputs[1][rows, :] = piece[height : 2 * height]
        outputs[3][rows, :] = piece[2 * height :]
    outputs[2][...] = factor_ref[...] + outputs[3][...]


def chip_sum_kernel(keep_ref, got_ref, *refs):
    outputs, total_ref = refs[:-1], refs[-1]
    total_ref[...] = keep_ref[...] + got_ref[...]
    height = outputs[0].shape[0]
    chip = lax.axis_index("wide") // 2
    for m, out in enumerate(outputs):
        out[...] = total_ref[pl.ds(pl.multiple_of((chip ^ m) * height, height), height), :]


def sum_kernel(*refs):
    total = refs[0][...]
    for x in refs[1:-1]:
        total = total + x[...]
    refs[-1][...] = total


def add_up(pieces):
    (total,) = kernel_call(sum_kernel, [shape(pieces[0].shape)], *pieces)
    return total


def sum_everywhere(give, keep):
    chips = lax.axis_size("wide") // 2
    half, rank = keep.shape
    got = swap(give, "wide", 1)
    pieces = kernel_call(
        chip_sum_kernel, [shape((half // chips, rank))] * chips, keep, got,
        scratch=[pltpu.VMEM((half, rank), jnp.float32)],
    )
    pieces = [pieces[0]] + [swap(pieces[m], "wide", 2 * m) for m in range(1, chips)]
    mine = add_up(pieces)
    mine = add_up(swaps([mine] * lax.axis_size("narrow")))
    pieces = [mine] + [swap(mine, "wide", 2 * m) for m in range(1, chips)]
    return [x for a in pieces for x in (a, swap(a, "wide", 1))]


def pick_kernel(count, table_ref, *refs):
    blocks, outputs = refs[:-count], refs[-count:]
    for d, out in enumerate(outputs):
        here = table_ref[d : d + 1, :1].astype(jnp.float32).astype(out.dtype)
        here = jnp.broadcast_to(here, out.shape)
        value = blocks[0][...]
        for r in range(1, len(blocks)):
            value = jnp.where(here == r, blocks[r][...], value)
        out[...] = value


def fetch_rows(lowered, table):
    chips = lax.axis_size("wide") // 2
    same = [lowered] + [swap(lowered, "wide", 2 * m) for m in range(1, chips)]
    blocks = [x for a in same for x in (a, swap(a, "wide", 1))]
    count = lax.axis_size("narrow")
    picked = kernel_call(
        functools.partial(pick_kernel, count), [shape(lowered.shape, lowered.dtype)] * count,
        table, *blocks,
    )
    return swaps(picked)


def tile_kernel(forward, count, activity_ref, time_ref, *refs):
    pieces, outputs = refs[:count], refs[count : 2 * count]
    tile_ref, stage_ref, sums_ref, sems = refs[2 * count :]
    steps = activity_ref.shape[1]
    copies = [
        pltpu.make_async_copy(activity_ref.at[0, k], tile_ref.at[k], sems.at[k])
        for k in range(steps)
    ]
    for copy in copies:
        copy.start()
    me = lax.axis_index("narrow")
    for d, piece in enumerate(pieces):
        stage_ref[me ^ d] = piece[...]
    low = jnp.concatenate([stage_ref[q] for q in range(count)], axis=0 if forward else 1)
    low = low.astype(jnp.float32)
    total = None
    for k in range(steps):
        khatri = (low * time_ref[:, k : k + 1]).astype(jnp.bfloat16)
        dims = (((1,), (1 if forward else 0,)), ((), ()))
        copies[k].wait()
        term = lax.dot_general(khatri, tile_ref[k], dims, preferred_element_type=jnp.float32)
        total = term if total is None else total + term
    width = outputs[0].shape[1]
    for q in range(count):
        sums_ref[q] = total[:, q * width : (q + 1) * width]
    for d, out in enumerate(outputs):
        out[...] = sums_ref[me ^ d]


def tile_sums(activity, pieces, time_by_rank, forward):
    count = len(pieces)
    rank = time_by_rank.shape[0]
    _, steps, rows, cols = activity.shape
    width = (rows if forward else cols) // count
    inside = pl.BlockSpec(memory_space=pltpu.VMEM)
    return pl.pallas_call(
        functools.partial(tile_kernel, forward, count),
        out_shape=(shape((rank, width)),) * count,
        in_specs=[pl.BlockSpec(memory_space=pl.ANY)] + [inside] * (count + 1),
        out_specs=(inside,) * count,
        scratch_shapes=[
            pltpu.VMEM(activity.shape[1:], activity.dtype),
            pltpu.VMEM((count, *pieces[0].shape), jnp.bfloat16),
            pltpu.VMEM((count, rank, width), jnp.float32),
            pltpu.SemaphoreType.DMA((steps,)),
        ],
        compiler_params=pltpu.CompilerParams(vmem_limit_bytes=60 * 2**20),
        cost_estimate=pl.CostEstimate(
            flops=2_000_000_000, bytes_accessed=2 * activity.size, transcendentals=0
        ),
        name="tile",
    )(activity, time_by_rank, *pieces)


def place_kernel(count, table_ref, *refs):
    received, outputs = refs[:count], refs[count:]
    values = [x[...] for x in received]
    for r, out in enumerate(outputs):
        total = None
        for d, value in enumerate(values):
            here = jnp.broadcast_to(table_ref[d : d + 1, :1] == r, value.shape)
            term = jnp.where(here, value, 0.0)
            total = term if total is None else total + term
        out[...] = total


def owner_sums(partials, table):
    received = swaps(partials)
    size = lax.axis_size("wide")
    placed = kernel_call(
        functools.partial(place_kernel, len(received)), [shape(received[0].shape)] * size,
        table, *received,
    )
    arrived = [swap(placed[2 * m + 1], "wide", 1) for m in range(1, size // 2)]
    terms = [placed[0], swap(placed[1], "wide", 1)]
    for m in range(1, size // 2):
        terms.append(swap(placed[2 * m] + arrived[m - 1], "wide", 2 * m))
    return terms


def update_kernel(terms, count, *refs):
    sums = refs[0][...]
    for term in refs[1:terms]:
        sums = sums + term[...]
    shifted_ref, dual_ref, penalty_ref, inverse_ref = refs[terms : terms + 4]
    outputs = refs[terms + 4 :]
    value_ref = outputs[-1]
    penalty = penalty_ref[:1, :1]
    inverse = inverse_ref[...]
    shifted, dual = shifted_ref[...], dual_ref[...]
    for _ in range(PASSES):
        target = jnp.dot(
            inverse, sums + penalty * shifted, precision=HIGHEST, preferred_element_type=jnp.float32
        )
        value = target - dual
        dual = jnp.maximum(-value, 0.0)
        shifted = jnp.abs(value)
    value_ref[...] = value
    height = outputs[0].shape[0]
    for d in range(count):
        outputs[d][...] = value_ref[rows_of(d, height), :]
    if len(outputs) > count + 1:
        low_ref, give_ref, keep_ref = outputs[count : count + 3]
        fresh = jnp.maximum(value, 0.0)
        low_ref[...] = fresh.astype(low_ref.dtype)
        halves(gram_of(fresh), give_ref, keep_ref)


def admm(terms, shifted, dual, penalty, inverse, more):
    count = lax.axis_size("narrow")
    rank, width = shifted.shape
    out = [shape((rank // count, width))] * count
    if more:
        out += [shape((rank, width), jnp.bfloat16)] + [shape((rank // 2, rank))] * 2
    return kernel_call(
        functools.partial(update_kernel, len(terms), count), out,
        *terms, shifted, dual, penalty, inverse,
        scratch=[pltpu.VMEM((rank, width), jnp.float32)],
        flops=12 * rank * rank * width * PASSES,
    )


def final_kernel(count, *refs):
    pieces, (factor_ref, dual_ref) = refs[:count], refs[count:]
    width = pieces[0].shape[1]

    def body(v):
        for d, piece in enumerate(pieces):
            lanes = slice((v ^ d) * width, ((v ^ d) + 1) * width)
            value = piece[...]
            factor_ref[:, lanes] = jnp.maximum(value, 0.0)
            dual_ref[:, lanes] = jnp.maximum(-value, 0.0)

    for_each_position(body)


def to_columns(pieces):
    received = swaps(pieces)
    height, width = received[0].shape
    count = len(received)
    factor, dual = kernel_call(
        functools.partial(final_kernel, count), [shape((height, count * width))] * 2,
        *received,
    )
    return factor.T, dual.T


def local(
    activity,
    tile_coords,
    user_owner,
    item_owner,
    user_factor,
    item_factor,
    time_factor,
    user_dual,
    item_dual,
):
    return sweep(
        activity, tile_coords, user_owner, item_owner, user_factor.T, item_factor.T,
        time_factor, user_dual.T, item_dual.T,
    )


def sweep(
    activity, tile_coords, user_owner, item_owner, user_factor, item_factor, time_factor,
    user_dual, item_dual,
):
    rank = time_factor.shape[1]
    time_by_rank = time_factor.T
    low, item_pieces = start(item_factor)
    user_table, item_table = positions(tile_coords, user_owner, item_owner)

    item_pieces = swaps(item_pieces)
    width = item_pieces[0].shape[1]
    item_rows, *gram = kernel_call(
        gram_kernel, [shape((rank, width))] + [shape((rank // 2, rank))] * 2, *item_pieces,
        flops=12 * rank * rank * width,
    )
    other_pieces = swaps(split(user_factor, user_dual, item_dual))
    user_shifted, udual_rows, item_shifted, idual_rows = kernel_call(
        assemble_kernel, [shape((rank, width))] * 4, item_rows, *other_pieces
    )

    partials = tile_sums(activity, fetch_rows(low, item_table), time_by_rank, True)
    terms = owner_sums(partials, user_table)
    penalty, inverse = penalty_inverse(sum_everywhere(*gram), time_factor)
    *user_pieces, low, give, keep = admm(terms, user_shifted, udual_rows, penalty, inverse, True)

    partials = tile_sums(activity, fetch_rows(low, user_table), time_by_rank, False)
    terms = owner_sums(partials, item_table)
    penalty, inverse = penalty_inverse(sum_everywhere(give, keep), time_factor)
    new_users, new_user_dual = to_columns(user_pieces)
    item_pieces = admm(terms, item_shifted, idual_rows, penalty, inverse, False)
    new_items, new_item_dual = to_columns(item_pieces)
    return (new_users, new_items, new_user_dual, new_item_dual)


def solution(mesh):
    in_specs = (
        P(("wide", "narrow"), None, None, None),
        P(),
        P(),
        P(),
        P("wide", "narrow"),
        P("wide", "narrow"),
        P(),
        P("wide", "narrow"),
        P("wide", "narrow"),
    )
    out_specs = (P("wide", "narrow"), P("wide", "narrow"), P("wide", "narrow"), P("wide", "narrow"))
    return jax.shard_map(local, mesh=mesh, in_specs=in_specs, out_specs=out_specs, check_vma=False)
```

profile of v0, /device:TPU:0, one launch (start us, length us, event | category | flops | bytes accessed | tf_op | source)
XLA Modules:
  0.0 163.2 jit_solution(2882354626474873733)
XLA Ops:
  0.6 0.9 copy-done.3
  1.6 3.1 %collective-permute-start.20 = (f32[64,128]{1,0:T(8,128)S(1)}, f32[64,128]{1,0:T(8,128)S(1)}, u32[]{:S(2)}, u32[]{:S(2)}) collective-permute-start(f32[64,128]{1,0:T(8,128)S(1)} %get-tuple-element.97), channel_id=1, source_target_pairs={{0,1},{1,0},{2,3},{3,2},{4,5},{5,4},{6,7},{7,6},{8,9},{9,8},{10,11... | collective-permute-start | bytes 98312 | tf_op jit(solution)/shard_map/ppermute | solution.py:128
  4.7 2.6 %collective-permute-start.21 = (f32[64,128]{1,0:T(8,128)S(1)}, f32[64,128]{1,0:T(8,128)S(1)}, u32[]{:S(2)}, u32[]{:S(2)}) collective-permute-start(f32[64,128]{1,0:T(8,128)S(1)} %get-tuple-element.98), channel_id=1, source_target_pairs={{0,2},{1,3},{2,0},{3,1},{4,6},{5,7},{6,4},{7,5},{8,10},{9,11},{10,... | collective-permute-start | bytes 98312 | tf_op jit(solution)/shard_map/ppermute | solution.py:128
  7.3 2.8 %collective-permute-done.21.refs_2_ = f32[64,128]{1,0:T(8,128)S(1)} collective-permute-done((f32[64,128]{1,0:T(8,128)S(1)}, f32[64,128]{1,0:T(8,128)S(1)}, u32[]{:S(2)}, u32[]{:S(2)}) %collective-permute-start.21) | collective-permute-done | bytes 32800 | tf_op jit(solution)/shard_map/ppermute | solution.py:128
  10.1 2.9 %collective-permute-done.22.refs_3_ = f32[64,128]{1,0:T(8,128)S(1)} collective-permute-done((f32[64,128]{1,0:T(8,128)S(1)}, f32[64,128]{1,0:T(8,128)S(1)}, u32[]{:S(2)}, u32[]{:S(2)}) %collective-permute-start.22) | collective-permute-done | bytes 32800 | tf_op jit(solution)/shard_map/ppermute | solution.py:128
  13.5 1.6 collective-permute-start.1
  15.0 1.5 collective-permute-start.3
  17.0 0.9 collective-permute-done.1.refs_2_
  21.8 0.9 copy-done.1
  22.7 0.9 copy-done.2
  24.4 1.6 collective-permute-start.27
  26.0 1.5 collective-permute-start.28
  27.7 1.9 %collective-permute-start.7 = (bf16[64,512]{1,0:T(8,128)(2,1)S(1)}, bf16[64,512]{1,0:T(8,128)(2,1)S(1)}, u32[]{:S(2)}, u32[]{:S(2)}) collective-permute-start(bf16[64,512]{1,0:T(8,128)(2,1)S(1)} %get-tuple-element.81), channel_id=1, source_target_pairs={{0,1},{1,0},{2,3},{3,2},{4,5},{5,4},{6,7},{7,6},{8,9},{9,8},{10,11... | collective-permute-start | bytes 196616 | tf_op jit(solution)/shard_map/ppermute | solution.py:128
  29.6 2.5 %collective-permute-start.9 = (bf16[64,512]{1,0:T(8,128)(2,1)S(1)}, bf16[64,512]{1,0:T(8,128)(2,1)S(1)}, u32[]{:S(2)}, u32[]{:S(2)}) collective-permute-start(bf16[64,512]{1,0:T(8,128)(2,1)S(1)} %get-tuple-element.83), channel_id=1, source_target_pairs={{0,3},{1,2},{2,1},{3,0},{4,7},{5,6},{6,5},{7,4},{8,11},{9,10},{10,... | collective-permute-start | bytes 196616 | tf_op jit(solution)/shard_map/ppermute | solution.py:128
  32.6 1.5 copy.14
  34.1 2.9 %collective-permute-done.29.refs_3_ = f32[32,256]{1,0:T(8,128)S(1)} collective-permute-done((f32[32,256]{1,0:T(8,128)S(1)}, f32[32,256]{1,0:T(8,128)S(1)}, u32[]{:S(2)}, u32[]{:S(2)}) %collective-permute-start.29) | collective-permute-done | bytes 32800 | tf_op jit(solution)/shard_map/ppermute | solution.py:128
  37.4 2.9 %collective-permute-start.25 = (f32[192,128]{1,0:T(8,128)S(1)}, f32[192,128]{1,0:T(8,128)S(1)}, u32[]{:S(2)}, u32[]{:S(2)}) collective-permute-start(f32[192,128]{1,0:T(8,128)S(1)} %get-tuple-element.104), channel_id=1, source_target_pairs={{0,3},{1,2},{2,1},{3,0},{4,7},{5,6},{6,5},{7,4},{8,11},{9,10},{10,... | collective-permute-start | bytes 294920 | tf_op jit(solution)/shard_map/ppermute | solution.py:128
  40.5 1.4 collective-permute-start.31
  41.9 2.9 %collective-permute-start.32 = (f32[32,256]{1,0:T(8,128)S(1)}, f32[32,256]{1,0:T(8,128)S(1)}, u32[]{:S(2)}, u32[]{:S(2)}) collective-permute-start(f32[32,256]{1,0:T(8,128)S(1)} %shard_map.128.refs_0_), channel_id=1, source_target_pairs={{0,3},{1,2},{2,1},{3,0},{4,7},{5,6},{6,5},{7,4},{8,11},{9,10},{10,... | collective-permute-start | bytes 98312 | tf_op jit(solution)/shard_map/ppermute | solution.py:128
  44.8 4.9 %tile.2 = (f32[256,128]{1,0:T(8,128)}, f32[256,128]{1,0:T(8,128)}, f32[256,128]{1,0:T(8,128)}, f32[256,128]{1,0:T(8,128)}) custom-call(bf16[1,8,512,512]{3,2,1,0:T(8,128)(2,1)} %activity_ref.3, f32[256,8]{1,0:T(8,128)} %bitcast.13, bf16[64,512]{1,0:T(8,128)(2,1)} %copy-done.9, bf16[64,512]{1,0:T(8,128)(2,1)} %copy-done.11, bf16[64,512]{1,0:T(8,128)(2,1)} %copy-done.12, ...), custom_call_target="tpu_custom_call" | custom-call | flops 2000000000 | bytes 4194304 | tf_op jit(solution)/shard_map/tile/pallas_call | solution.py:332
  49.8 1.5 collective-permute-start.11
  51.4 2.8 %collective-permute-start.12 = (f32[256,128]{1,0:T(8,128)}, f32[256,128]{1,0:T(8,128)S(1)}, u32[]{:S(2)}, u32[]{:S(2)}) collective-permute-start(f32[256,128]{1,0:T(8,128)} %get-tuple-element.87), channel_id=1, source_target_pairs={{0,3},{1,2},{2,1},{3,0},{4,7},{5,6},{6,5},{7,4},{8,11},{9,10},{10,... | collective-permute-start | bytes 393224 | tf_op jit(solution)/shard_map/ppermute | solution.py:128
  55.3 2.9 %collective-permute-done.34.refs_2_ = f32[32,256]{1,0:T(8,128)S(1)} collective-permute-done((f32[32,256]{1,0:T(8,128)S(1)}, f32[32,256]{1,0:T(8,128)S(1)}, u32[]{:S(2)}, u32[]{:S(2)}) %collective-permute-start.34) | collective-permute-done | bytes 32800 | tf_op jit(solution)/shard_map/ppermute | solution.py:128
  58.7 4.3 %collective-permute-done.38.refs_6_ = f32[32,256]{1,0:T(8,128)S(1)} collective-permute-done((f32[32,256]{1,0:T(8,128)S(1)}, f32[32,256]{1,0:T(8,128)S(1)}, u32[]{:S(2)}, u32[]{:S(2)}) %collective-permute-start.38) | collective-permute-done | bytes 32800 | tf_op jit(solution)/shard_map/ppermute | solution.py:128
  66.0 4.9 %shard_map.130 = (f32[256,256]{1,0:T(8,128)S(1)}, f32[1,128]{1,0:T(1,128)S(1)}) custom-call(f32[8,256]{1,0:T(8,128)S(1)} %copy-done.6, f32[32,256]{1,0:T(8,128)S(1)} %shard_map.129.refs_0_, f32[32,256]{1,0:T(8,128)S(1)} %collective-permute-done.33.refs_1_, f32[32,256]{1,0:T(8,128)S(1)} %collective-permute-done.34.refs_2_, ...), custom_call_target="tpu_custom_call" | custom-call | flops 6000000000 | bytes 532992 | tf_op jit(solution)/shard_map/pallas_call | solution.py:111
  71.7 1.6 collective-permute-start.17
  73.3 1.5 collective-permute-start.15
  74.9 4.4 %shard_map.131.refs_8_ = f32[256,256]{1,0:T(8,128)S(1)} custom-call(f32[256,256]{1,0:T(8,128)S(1)} %get-tuple-element.114.half_ref), custom_call_target="tpu_custom_call" | custom-call | flops 6000000000 | bytes 524288 | tf_op jit(solution)/shard_map/pallas_call | solution.py:111
  80.1 1.5 shard_map.132
  81.7 1.2 collective-permute-start.44
  83.5 1.7 %collective-permute-start.48 = (bf16[256,128]{1,0:T(8,128)(2,1)S(1)}, bf16[256,128]{1,0:T(8,128)(2,1)S(1)}, u32[]{:S(2)}, u32[]{:S(2)}) collective-permute-start(bf16[256,128]{1,0:T(8,128)(2,1)S(1)} %get-tuple-element.120.refs_0_), channel_id=1, source_target_pairs={{0,24},{4,28},{8,16},{12,20},{16,8},{20,12},{24,0},{28,4},{1,25},{... | collective-permute-start | bytes 196616 | tf_op jit(solution)/shard_map/ppermute | solution.py:128
  85.3 0.9 collective-permute-done.44.refs_2_
  86.2 1.7 %collective-permute-done.46.refs_4_ = bf16[256,128]{1,0:T(8,128)(2,1)S(1)} collective-permute-done((bf16[256,128]{1,0:T(8,128)(2,1)S(1)}, bf16[256,128]{1,0:T(8,128)(2,1)S(1)}, u32[]{:S(2)}, u32[]{:S(2)}) %collective-permute-start.46) | collective-permute-done | bytes 65568 | tf_op jit(solution)/shard_map/ppermute | solution.py:128
  88.7 1.6 collective-permute-start.64
  91.2 2.2 %collective-permute-start.51 = (bf16[256,128]{1,0:T(8,128)(2,1)S(1)}, bf16[256,128]{1,0:T(8,128)(2,1)S(1)}, u32[]{:S(2)}, u32[]{:S(2)}) collective-permute-start(bf16[256,128]{1,0:T(8,128)(2,1)S(1)} %get-tuple-element.123), channel_id=1, source_target_pairs={{0,2},{1,3},{2,0},{3,1},{4,6},{5,7},{6,4},{7,5},{8,10},{9,11},{10,... | collective-permute-start | bytes 196616 | tf_op jit(solution)/shard_map/ppermute | solution.py:128
  93.4 2.2 %collective-permute-start.52 = (bf16[256,128]{1,0:T(8,128)(2,1)S(1)}, bf16[256,128]{1,0:T(8,128)(2,1)S(1)}, u32[]{:S(2)}, u32[]{:S(2)}) collective-permute-start(bf16[256,128]{1,0:T(8,128)(2,1)S(1)} %get-tuple-element.124), channel_id=1, source_target_pairs={{0,3},{1,2},{2,1},{3,0},{4,7},{5,6},{6,5},{7,4},{8,11},{9,10},{10,... | collective-permute-start | bytes 196616 | tf_op jit(solution)/shard_map/ppermute | solution.py:128
  95.6 1.1 collective-permute-start.65
  96.6 1.5 collective-permute-start.66
  98.2 1.7 %collective-permute-done.65.refs_2_ = f32[32,256]{1,0:T(8,128)S(1)} collective-permute-done((f32[32,256]{1,0:T(8,128)S(1)}, f32[32,256]{1,0:T(8,128)S(1)}, u32[]{:S(2)}, u32[]{:S(2)}) %collective-permute-start.65) | collective-permute-done | bytes 32800 | tf_op jit(solution)/shard_map/ppermute | solution.py:128
  99.8 1.6 collective-permute-done.66.refs_3_
  102.3 4.7 %tile.3 = (f32[256,128]{1,0:T(8,128)}, f32[256,128]{1,0:T(8,128)}, f32[256,128]{1,0:T(8,128)}, f32[256,128]{1,0:T(8,128)}) custom-call(bf16[1,8,512,512]{3,2,1,0:T(8,128)(2,1)} %activity_ref.3, f32[256,8]{1,0:T(8,128)} %bitcast.14, bf16[256,128]{1,0:T(8,128)(2,1)} %copy-done.10, bf16[256,128]{1,0:T(8,128)(2,1)} %copy-done.14, bf16[256,128]{1,0:T(8,128)(2,1)} %copy-done.15, ...), custom_call_target="tpu_custom_call" | custom-call | flops 2000000000 | bytes 4194304 | tf_op jit(solution)/shard_map/tile/pallas_call | solution.py:332
  107.0 2.1 %collective-permute-start.53 = (f32[256,128]{1,0:T(8,128)}, f32[256,128]{1,0:T(8,128)S(1)}, u32[]{:S(2)}, u32[]{:S(2)}) collective-permute-start(f32[256,128]{1,0:T(8,128)} %get-tuple-element.126), channel_id=1, source_target_pairs={{0,1},{1,0},{2,3},{3,2},{4,5},{5,4},{6,7},{7,6},{8,9},{9,8},{10,11... | collective-permute-start | bytes 393224 | tf_op jit(solution)/shard_map/ppermute | solution.py:128
  109.1 2.4 %collective-permute-start.55 = (f32[256,128]{1,0:T(8,128)}, f32[256,128]{1,0:T(8,128)S(1)}, u32[]{:S(2)}, u32[]{:S(2)}) collective-permute-start(f32[256,128]{1,0:T(8,128)} %get-tuple-element.128), channel_id=1, source_target_pairs={{0,3},{1,2},{2,1},{3,0},{4,7},{5,6},{6,5},{7,4},{8,11},{9,10},{10,... | collective-permute-start | bytes 393224 | tf_op jit(solution)/shard_map/ppermute | solution.py:128
  111.5 0.9 collective-permute-start.68
  112.4 2.5 %collective-permute-start.69 = (f32[32,256]{1,0:T(8,128)S(1)}, f32[32,256]{1,0:T(8,128)S(1)}, u32[]{:S(2)}, u32[]{:S(2)}) collective-permute-start(f32[32,256]{1,0:T(8,128)S(1)} %shard_map.137.refs_0_), channel_id=1, source_target_pairs={{0,3},{1,2},{2,1},{3,0},{4,7},{5,6},{6,5},{7,4},{8,11},{9,10},{10,... | collective-permute-start | bytes 98312 | tf_op jit(solution)/shard_map/ppermute | solution.py:128
  114.9 9.2 %collective-permute-done.68.refs_2_ = f32[32,256]{1,0:T(8,128)S(1)} collective-permute-done((f32[32,256]{1,0:T(8,128)S(1)}, f32[32,256]{1,0:T(8,128)S(1)}, u32[]{:S(2)}, u32[]{:S(2)}) %collective-permute-start.68) | collective-permute-done | bytes 32800 | tf_op jit(solution)/shard_map/ppermute | solution.py:128
  124.1 1.0 collective-permute-start.71
  125.2 1.1 collective-permute-start.73
  126.3 1.8 %collective-permute-done.71.refs_2_ = f32[32,256]{1,0:T(8,128)S(1)} collective-permute-done((f32[32,256]{1,0:T(8,128)S(1)}, f32[32,256]{1,0:T(8,128)S(1)}, u32[]{:S(2)}, u32[]{:S(2)}) %collective-permute-start.71) | collective-permute-done | bytes 32800 | tf_op jit(solution)/shard_map/ppermute | solution.py:128
  128.1 1.5 collective-permute-start.75
  129.6 3.3 %collective-permute-done.75.refs_6_ = f32[32,256]{1,0:T(8,128)S(1)} collective-permute-done((f32[32,256]{1,0:T(8,128)S(1)}, f32[32,256]{1,0:T(8,128)S(1)}, u32[]{:S(2)}, u32[]{:S(2)}) %collective-permute-start.75) | collective-permute-done | bytes 32800 | tf_op jit(solution)/shard_map/ppermute | solution.py:128
  133.5 0.9 collective-permute-start.40
  134.4 0.9 copy-done.5
  136.5 4.9 %shard_map.139 = (f32[256,256]{1,0:T(8,128)S(1)}, f32[1,128]{1,0:T(1,128)S(1)}) custom-call(f32[8,256]{1,0:T(8,128)S(1)} %copy-done.6, f32[32,256]{1,0:T(8,128)S(1)} %shard_map.138.refs_0_, f32[32,256]{1,0:T(8,128)S(1)} %collective-permute-done.70.refs_1_, f32[32,256]{1,0:T(8,128)S(1)} %collective-permute-done.71.refs_2_, ...), custom_call_target="tpu_custom_call" | custom-call | flops 6000000000 | bytes 532992 | tf_op jit(solution)/shard_map/pallas_call | solution.py:111
  141.9 1.6 collective-permute-start.62
  143.5 1.0 collective-permute-start.60
  144.5 1.1 collective-permute-start.58
  145.6 4.4 %shard_map.140.refs_8_ = f32[256,256]{1,0:T(8,128)S(1)} custom-call(f32[256,256]{1,0:T(8,128)S(1)} %get-tuple-element.146.half_ref), custom_call_target="tpu_custom_call" | custom-call | flops 6000000000 | bytes 524288 | tf_op jit(solution)/shard_map/pallas_call | solution.py:111
  150.1 1.1 collective-permute-start.41
  151.1 2.5 %collective-permute-start.42 = (f32[64,128]{1,0:T(8,128)S(1)}, f32[64,128]{1,0:T(8,128)S(1)}, u32[]{:S(2)}, u32[]{:S(2)}) collective-permute-start(f32[64,128]{1,0:T(8,128)S(1)} %get-tuple-element.118), channel_id=1, source_target_pairs={{0,3},{1,2},{2,1},{3,0},{4,7},{5,6},{6,5},{7,4},{8,11},{9,10},{10,... | collective-permute-start | bytes 98312 | tf_op jit(solution)/shard_map/ppermute | solution.py:128
  153.6 1.2 shard_map.141
  154.9 1.9 %collective-permute-start.78 = (f32[64,128]{1,0:T(8,128)S(1)}, f32[64,128]{1,0:T(8,128)S(1)}, u32[]{:S(2)}, u32[]{:S(2)}) collective-permute-start(f32[64,128]{1,0:T(8,128)S(1)} %get-tuple-element.149), channel_id=1, source_target_pairs={{0,2},{1,3},{2,0},{3,1},{4,6},{5,7},{6,4},{7,5},{8,10},{9,11},{10,... | collective-permute-start | bytes 98312 | tf_op jit(solution)/shard_map/ppermute | solution.py:128
  156.8 2.5 %collective-permute-start.79 = (f32[64,128]{1,0:T(8,128)S(1)}, f32[64,128]{1,0:T(8,128)S(1)}, u32[]{:S(2)}, u32[]{:S(2)}) collective-permute-start(f32[64,128]{1,0:T(8,128)S(1)} %get-tuple-element.150), channel_id=1, source_target_pairs={{0,3},{1,2},{2,1},{3,0},{4,7},{5,6},{6,5},{7,4},{8,11},{9,10},{10,... | collective-permute-start | bytes 98312 | tf_op jit(solution)/shard_map/ppermute | solution.py:128
  160.1 2.4 %collective-permute-done.79.refs_3_ = f32[64,128]{1,0:T(8,128)S(1)} collective-permute-done((f32[64,128]{1,0:T(8,128)S(1)}, f32[64,128]{1,0:T(8,128)S(1)}, u32[]{:S(2)}, u32[]{:S(2)}) %collective-permute-start.79) | collective-permute-done | bytes 32800 | tf_op jit(solution)/shard_map/ppermute | solution.py:128
  (164 shorter events, 20.1 us)
Async XLA Ops:
  1.6 5.7 %collective-permute-start.20 = (f32[64,128]{1,0:T(8,128)S(1)}, f32[64,128]{1,0:T(8,128)S(1)}, u32[]{:S(2)}, u32[]{:S(2)}) collective-permute-start(f32[64,128]{1,0:T(8,128)S(1)} %get-tuple-element.97), channel_id=1, source_target_pairs={{0,1},{1,0},{2,3},{3,2},{4,5},{5,4},{6,7},{7,6},{8,9},{9,8},{10,11... | collective-permute-start | bytes 98312 | tf_op jit(solution)/shard_map/ppermute | solution.py:128
  4.7 5.4 %collective-permute-start.21 = (f32[64,128]{1,0:T(8,128)S(1)}, f32[64,128]{1,0:T(8,128)S(1)}, u32[]{:S(2)}, u32[]{:S(2)}) collective-permute-start(f32[64,128]{1,0:T(8,128)S(1)} %get-tuple-element.98), channel_id=1, source_target_pairs={{0,2},{1,3},{2,0},{3,1},{4,6},{5,7},{6,4},{7,5},{8,10},{9,11},{10,... | collective-permute-start | bytes 98312 | tf_op jit(solution)/shard_map/ppermute | solution.py:128
  7.3 5.7 %collective-permute-start.22 = (f32[64,128]{1,0:T(8,128)S(1)}, f32[64,128]{1,0:T(8,128)S(1)}, u32[]{:S(2)}, u32[]{:S(2)}) collective-permute-start(f32[64,128]{1,0:T(8,128)S(1)} %get-tuple-element.99), channel_id=1, source_target_pairs={{0,3},{1,2},{2,1},{3,0},{4,7},{5,6},{6,5},{7,4},{8,11},{9,10},{10,... | collective-permute-start | bytes 98312 | tf_op jit(solution)/shard_map/ppermute | solution.py:128
  13.4 10.9 %collective-permute-start.26 = (f32[128,256]{1,0:T(8,128)S(1)}, f32[128,256]{1,0:T(8,128)S(1)}, u32[]{:S(2)}, u32[]{:S(2)}) collective-permute-start(f32[128,256]{1,0:T(8,128)S(1)} %get-tuple-element.108), channel_id=1, source_target_pairs={{0,4},{4,0},{8,12},{12,8},{16,20},{20,16},{24,28},{28,24},{1,5},{5... | collective-permute-start | bytes 393224 | tf_op jit(solution)/shard_map/ppermute | solution.py:128
  13.5 4.5 %collective-permute-start.1 = (bf16[64,512]{1,0:T(8,128)(2,1)S(1)}, bf16[64,512]{1,0:T(8,128)(2,1)S(1)}, u32[]{:S(2)}, u32[]{:S(2)}) collective-permute-start(bf16[64,512]{1,0:T(8,128)(2,1)S(1)} %get-tuple-element.79.refs_0_), channel_id=1, source_target_pairs={{0,8},{4,12},{8,0},{12,4},{16,24},{20,28},{24,16},{28,20},{1,9},{5... | collective-permute-start | bytes 196616 | tf_op jit(solution)/shard_map/ppermute | solution.py:128
  15.0 8.6 %collective-permute-start.3 = (bf16[64,512]{1,0:T(8,128)(2,1)S(1)}, bf16[64,512]{1,0:T(8,128)(2,1)S(1)}, u32[]{:S(2)}, u32[]{:S(2)}) collective-permute-start(bf16[64,512]{1,0:T(8,128)(2,1)S(1)} %get-tuple-element.79.refs_0_), channel_id=1, source_target_pairs={{0,16},{4,20},{8,24},{12,28},{16,0},{20,4},{24,8},{28,12},{1,17},{... | collective-permute-start | bytes 196616 | tf_op jit(solution)/shard_map/ppermute | solution.py:128
  16.5 7.2 %collective-permute-start.5 = (bf16[64,512]{1,0:T(8,128)(2,1)S(1)}, bf16[64,512]{1,0:T(8,128)(2,1)S(1)}, u32[]{:S(2)}, u32[]{:S(2)}) collective-permute-start(bf16[64,512]{1,0:T(8,128)(2,1)S(1)} %get-tuple-element.79.refs_0_), channel_id=1, source_target_pairs={{0,24},{4,28},{8,16},{12,20},{16,8},{20,12},{24,0},{28,4},{1,25},{... | collective-permute-start | bytes 196616 | tf_op jit(solution)/shard_map/ppermute | solution.py:128
  17.0 7.4 %collective-permute-start = (bf16[64,512]{1,0:T(8,128)(2,1)S(1)}, bf16[64,512]{1,0:T(8,128)(2,1)S(1)}, u32[]{:S(2)}, u32[]{:S(2)}) collective-permute-start(bf16[64,512]{1,0:T(8,128)(2,1)S(1)} %get-tuple-element.79.refs_0_), channel_id=1, source_target_pairs={{0,4},{4,0},{8,12},{12,8},{16,20},{20,16},{24,28},{28,24},{1,5},{5... | collective-permute-start | bytes 196616 | tf_op jit(solution)/shard_map/ppermute | solution.py:128
  18.0 8.0 %collective-permute-start.2 = (bf16[64,512]{1,0:T(8,128)(2,1)S(1)}, bf16[64,512]{1,0:T(8,128)(2,1)S(1)}, u32[]{:S(2)}, u32[]{:S(2)}) collective-permute-start(bf16[64,512]{1,0:T(8,128)(2,1)S(1)} %collective-permute-done.1.refs_2_), channel_id=1, source_target_pairs={{0,4},{4,0},{8,12},{12,8},{16,20},{20,16},{24,28},{28,24},{1,5},{5... | collective-permute-start | bytes 196616 | tf_op jit(solution)/shard_map/ppermute | solution.py:128
  23.7 13.8 %collective-permute-start.23 = (f32[192,128]{1,0:T(8,128)S(1)}, f32[192,128]{1,0:T(8,128)S(1)}, u32[]{:S(2)}, u32[]{:S(2)}) collective-permute-start(f32[192,128]{1,0:T(8,128)S(1)} %get-tuple-element.102), channel_id=1, source_target_pairs={{0,1},{1,0},{2,3},{3,2},{4,5},{5,4},{6,7},{7,6},{8,9},{9,8},{10,11... | collective-permute-start | bytes 294920 | tf_op jit(solution)/shard_map/ppermute | solution.py:128
  24.4 5.2 %collective-permute-start.27 = (f32[32,256]{1,0:T(8,128)S(1)}, f32[32,256]{1,0:T(8,128)S(1)}, u32[]{:S(2)}, u32[]{:S(2)}) collective-permute-start(f32[32,256]{1,0:T(8,128)S(1)} %get-tuple-element.110), channel_id=1, source_target_pairs={{0,8},{4,12},{8,0},{12,4},{16,24},{20,28},{24,16},{28,20},{1,9},{5... | collective-permute-start | bytes 98312 | tf_op jit(solution)/shard_map/ppermute | solution.py:128
  26.0 6.1 %collective-permute-start.28 = (f32[32,256]{1,0:T(8,128)S(1)}, f32[32,256]{1,0:T(8,128)S(1)}, u32[]{:S(2)}, u32[]{:S(2)}) collective-permute-start(f32[32,256]{1,0:T(8,128)S(1)} %get-tuple-element.111), channel_id=1, source_target_pairs={{0,16},{4,20},{8,24},{12,28},{16,0},{20,4},{24,8},{28,12},{1,17},{... | collective-permute-start | bytes 98312 | tf_op jit(solution)/shard_map/ppermute | solution.py:128
  27.7 12.7 %collective-permute-start.7 = (bf16[64,512]{1,0:T(8,128)(2,1)S(1)}, bf16[64,512]{1,0:T(8,128)(2,1)S(1)}, u32[]{:S(2)}, u32[]{:S(2)}) collective-permute-start(bf16[64,512]{1,0:T(8,128)(2,1)S(1)} %get-tuple-element.81), channel_id=1, source_target_pairs={{0,1},{1,0},{2,3},{3,2},{4,5},{5,4},{6,7},{7,6},{8,9},{9,8},{10,11... | collective-permute-start | bytes 196616 | tf_op jit(solution)/shard_map/ppermute | solution.py:128
  29.6 10.9 %collective-permute-start.8 = (bf16[64,512]{1,0:T(8,128)(2,1)S(1)}, bf16[64,512]{1,0:T(8,128)(2,1)S(1)}, u32[]{:S(2)}, u32[]{:S(2)}) collective-permute-start(bf16[64,512]{1,0:T(8,128)(2,1)S(1)} %get-tuple-element.82), channel_id=1, source_target_pairs={{0,2},{1,3},{2,0},{3,1},{4,6},{5,7},{6,4},{7,5},{8,10},{9,11},{10,... | collective-permute-start | bytes 196616 | tf_op jit(solution)/shard_map/ppermute | solution.py:128
  29.6 12.3 %collective-permute-start.9 = (bf16[64,512]{1,0:T(8,128)(2,1)S(1)}, bf16[64,512]{1,0:T(8,128)(2,1)S(1)}, u32[]{:S(2)}, u32[]{:S(2)}) collective-permute-start(bf16[64,512]{1,0:T(8,128)(2,1)S(1)} %get-tuple-element.83), channel_id=1, source_target_pairs={{0,3},{1,2},{2,1},{3,0},{4,7},{5,6},{6,5},{7,4},{8,11},{9,10},{10,... | collective-permute-start | bytes 196616 | tf_op jit(solution)/shard_map/ppermute | solution.py:128
  32.1 4.8 %collective-permute-start.29 = (f32[32,256]{1,0:T(8,128)S(1)}, f32[32,256]{1,0:T(8,128)S(1)}, u32[]{:S(2)}, u32[]{:S(2)}) collective-permute-start(f32[32,256]{1,0:T(8,128)S(1)} %get-tuple-element.112), channel_id=1, source_target_pairs={{0,24},{4,28},{8,16},{12,20},{16,8},{20,12},{24,0},{28,4},{1,25},{... | collective-permute-start | bytes 98312 | tf_op jit(solution)/shard_map/ppermute | solution.py:128
  37.0 17.3 %collective-permute-start.24 = (f32[192,128]{1,0:T(8,128)S(1)}, f32[192,128]{1,0:T(8,128)S(1)}, u32[]{:S(2)}, u32[]{:S(2)}) collective-permute-start(f32[192,128]{1,0:T(8,128)S(1)} %get-tuple-element.103), channel_id=1, source_target_pairs={{0,2},{1,3},{2,0},{3,1},{4,6},{5,7},{6,4},{7,5},{8,10},{9,11},{10,... | collective-permute-start | bytes 294920 | tf_op jit(solution)/shard_map/ppermute | solution.py:128
  37.4 17.4 %collective-permute-start.25 = (f32[192,128]{1,0:T(8,128)S(1)}, f32[192,128]{1,0:T(8,128)S(1)}, u32[]{:S(2)}, u32[]{:S(2)}) collective-permute-start(f32[192,128]{1,0:T(8,128)S(1)} %get-tuple-element.104), channel_id=1, source_target_pairs={{0,3},{1,2},{2,1},{3,0},{4,7},{5,6},{6,5},{7,4},{8,11},{9,10},{10,... | collective-permute-start | bytes 294920 | tf_op jit(solution)/shard_map/ppermute | solution.py:128
  40.4 9.4 %collective-permute-start.30 = (f32[32,256]{1,0:T(8,128)S(1)}, f32[32,256]{1,0:T(8,128)S(1)}, u32[]{:S(2)}, u32[]{:S(2)}) collective-permute-start(f32[32,256]{1,0:T(8,128)S(1)} %shard_map.128.refs_0_), channel_id=1, source_target_pairs={{0,1},{1,0},{2,3},{3,2},{4,5},{5,4},{6,7},{7,6},{8,9},{9,8},{10,11... | collective-permute-start | bytes 98312 | tf_op jit(solution)/shard_map/ppermute | solution.py:128
  40.5 9.3 %collective-permute-start.31 = (f32[32,256]{1,0:T(8,128)S(1)}, f32[32,256]{1,0:T(8,128)S(1)}, u32[]{:S(2)}, u32[]{:S(2)}) collective-permute-start(f32[32,256]{1,0:T(8,128)S(1)} %shard_map.128.refs_0_), channel_id=1, source_target_pairs={{0,2},{1,3},{2,0},{3,1},{4,6},{5,7},{6,4},{7,5},{8,10},{9,11},{10,... | collective-permute-start | bytes 98312 | tf_op jit(solution)/shard_map/ppermute | solution.py:128
  41.9 9.4 %collective-permute-start.32 = (f32[32,256]{1,0:T(8,128)S(1)}, f32[32,256]{1,0:T(8,128)S(1)}, u32[]{:S(2)}, u32[]{:S(2)}) collective-permute-start(f32[32,256]{1,0:T(8,128)S(1)} %shard_map.128.refs_0_), channel_id=1, source_target_pairs={{0,3},{1,2},{2,1},{3,0},{4,7},{5,6},{6,5},{7,4},{8,11},{9,10},{10,... | collective-permute-start | bytes 98312 | tf_op jit(solution)/shard_map/ppermute | solution.py:128
  49.7 13.3 %collective-permute-start.10 = (f32[256,128]{1,0:T(8,128)}, f32[256,128]{1,0:T(8,128)S(1)}, u32[]{:S(2)}, u32[]{:S(2)}) collective-permute-start(f32[256,128]{1,0:T(8,128)} %get-tuple-element.85), channel_id=1, source_target_pairs={{0,1},{1,0},{2,3},{3,2},{4,5},{5,4},{6,7},{7,6},{8,9},{9,8},{10,11... | collective-permute-start | bytes 393224 | tf_op jit(solution)/shard_map/ppermute | solution.py:128
  49.8 13.7 %collective-permute-start.11 = (f32[256,128]{1,0:T(8,128)}, f32[256,128]{1,0:T(8,128)S(1)}, u32[]{:S(2)}, u32[]{:S(2)}) collective-permute-start(f32[256,128]{1,0:T(8,128)} %get-tuple-element.86), channel_id=1, source_target_pairs={{0,2},{1,3},{2,0},{3,1},{4,6},{5,7},{6,4},{7,5},{8,10},{9,11},{10,... | collective-permute-start | bytes 393224 | tf_op jit(solution)/shard_map/ppermute | solution.py:128
  51.4 12.3 %collective-permute-start.12 = (f32[256,128]{1,0:T(8,128)}, f32[256,128]{1,0:T(8,128)S(1)}, u32[]{:S(2)}, u32[]{:S(2)}) collective-permute-start(f32[256,128]{1,0:T(8,128)} %get-tuple-element.87), channel_id=1, source_target_pairs={{0,3},{1,2},{2,1},{3,0},{4,7},{5,6},{6,5},{7,4},{8,11},{9,10},{10,... | collective-permute-start | bytes 393224 | tf_op jit(solution)/shard_map/ppermute | solution.py:128
  58.2 4.8 %collective-permute-start.38 = (f32[32,256]{1,0:T(8,128)S(1)}, f32[32,256]{1,0:T(8,128)S(1)}, u32[]{:S(2)}, u32[]{:S(2)}) collective-permute-start(f32[32,256]{1,0:T(8,128)S(1)} %shard_map.129.refs_0_), channel_id=1, source_target_pairs={{0,24},{4,28},{8,16},{12,20},{16,8},{20,12},{24,0},{28,4},{1,25},{... | collective-permute-start | bytes 98312 | tf_op jit(solution)/shard_map/ppermute | solution.py:128
  58.7 6.7 %collective-permute-start.33 = (f32[32,256]{1,0:T(8,128)S(1)}, f32[32,256]{1,0:T(8,128)S(1)}, u32[]{:S(2)}, u32[]{:S(2)}) collective-permute-start(f32[32,256]{1,0:T(8,128)S(1)} %shard_map.129.refs_0_), channel_id=1, source_target_pairs={{0,4},{4,0},{8,12},{12,8},{16,20},{20,16},{24,28},{28,24},{1,5},{5... | collective-permute-start | bytes 98312 | tf_op jit(solution)/shard_map/ppermute | solution.py:128
  65.0 6.1 %collective-permute-start.18 = (f32[256,128]{1,0:T(8,128)S(1)}, f32[256,128]{1,0:T(8,128)S(1)}, u32[]{:S(2)}, u32[]{:S(2)}) collective-permute-start(f32[256,128]{1,0:T(8,128)S(1)} %get-tuple-element.95), channel_id=1, source_target_pairs={{0,4},{4,0},{8,12},{12,8},{16,20},{20,16},{24,28},{28,24},{1,5},{5... | collective-permute-start | bytes 393224 | tf_op jit(solution)/shard_map/ppermute | solution.py:128
  65.5 6.2 %collective-permute-start.16 = (f32[256,128]{1,0:T(8,128)S(1)}, f32[256,128]{1,0:T(8,128)S(1)}, u32[]{:S(2)}, u32[]{:S(2)}) collective-permute-start(f32[256,128]{1,0:T(8,128)S(1)} %get-tuple-element.93), channel_id=1, source_target_pairs={{0,4},{4,0},{8,12},{12,8},{16,20},{20,16},{24,28},{28,24},{1,5},{5... | collective-permute-start | bytes 393224 | tf_op jit(solution)/shard_map/ppermute | solution.py:128
  65.6 7.7 %collective-permute-start.14 = (f32[256,128]{1,0:T(8,128)S(1)}, f32[256,128]{1,0:T(8,128)S(1)}, u32[]{:S(2)}, u32[]{:S(2)}) collective-permute-start(f32[256,128]{1,0:T(8,128)S(1)} %get-tuple-element.91), channel_id=1, source_target_pairs={{0,4},{4,0},{8,12},{12,8},{16,20},{20,16},{24,28},{28,24},{1,5},{5... | collective-permute-start | bytes 393224 | tf_op jit(solution)/shard_map/ppermute | solution.py:128
  70.9 8.3 %collective-permute-start.13 = (f32[256,128]{1,0:T(8,128)S(1)}, f32[256,128]{1,0:T(8,128)S(1)}, u32[]{:S(2)}, u32[]{:S(2)}) collective-permute-start(f32[256,128]{1,0:T(8,128)S(1)} %get-tuple-element.89), channel_id=1, source_target_pairs={{0,4},{4,0},{8,12},{12,8},{16,20},{20,16},{24,28},{28,24},{1,5},{5... | collective-permute-start | bytes 393224 | tf_op jit(solution)/shard_map/ppermute | solution.py:128
  71.1 8.1 %collective-permute-start.19 = (f32[256,128]{1,0:T(8,128)S(1)}, f32[256,128]{1,0:T(8,128)S(1)}, u32[]{:S(2)}, u32[]{:S(2)}) collective-permute-start(f32[256,128]{1,0:T(8,128)S(1)} %add.20), channel_id=1, source_target_pairs={{0,24},{4,28},{8,16},{12,20},{16,8},{20,12},{24,0},{28,4},{1,25},{... | collective-permute-start | bytes 393224 | tf_op jit(solution)/shard_map/ppermute | solution.py:128
  71.7 8.4 %collective-permute-start.17 = (f32[256,128]{1,0:T(8,128)S(1)}, f32[256,128]{1,0:T(8,128)S(1)}, u32[]{:S(2)}, u32[]{:S(2)}) collective-permute-start(f32[256,128]{1,0:T(8,128)S(1)} %add.19), channel_id=1, source_target_pairs={{0,16},{4,20},{8,24},{12,28},{16,0},{20,4},{24,8},{28,12},{1,17},{... | collective-permute-start | bytes 393224 | tf_op jit(solution)/shard_map/ppermute | solution.py:128
  73.3 6.8 %collective-permute-start.15 = (f32[256,128]{1,0:T(8,128)S(1)}, f32[256,128]{1,0:T(8,128)S(1)}, u32[]{:S(2)}, u32[]{:S(2)}) collective-permute-start(f32[256,128]{1,0:T(8,128)S(1)} %add.18), channel_id=1, source_target_pairs={{0,8},{4,12},{8,0},{12,4},{16,24},{20,28},{24,16},{28,20},{1,9},{5... | collective-permute-start | bytes 393224 | tf_op jit(solution)/shard_map/ppermute | solution.py:128
  81.6 7.1 %collective-permute-start.63 = (f32[128,256]{1,0:T(8,128)S(1)}, f32[128,256]{1,0:T(8,128)S(1)}, u32[]{:S(2)}, u32[]{:S(2)}) collective-permute-start(f32[128,256]{1,0:T(8,128)S(1)} %get-tuple-element.140), channel_id=1, source_target_pairs={{0,4},{4,0},{8,12},{12,8},{16,20},{20,16},{24,28},{28,24},{1,5},{5... | collective-permute-start | bytes 393224 | tf_op jit(solution)/shard_map/ppermute | solution.py:128
  81.7 4.5 %collective-permute-start.44 = (bf16[256,128]{1,0:T(8,128)(2,1)S(1)}, bf16[256,128]{1,0:T(8,128)(2,1)S(1)}, u32[]{:S(2)}, u32[]{:S(2)}) collective-permute-start(bf16[256,128]{1,0:T(8,128)(2,1)S(1)} %get-tuple-element.120.refs_0_), channel_id=1, source_target_pairs={{0,8},{4,12},{8,0},{12,4},{16,24},{20,28},{24,16},{28,20},{1,9},{5... | collective-permute-start | bytes 196616 | tf_op jit(solution)/shard_map/ppermute | solution.py:128
  82.9 5.0 %collective-permute-start.46 = (bf16[256,128]{1,0:T(8,128)(2,1)S(1)}, bf16[256,128]{1,0:T(8,128)(2,1)S(1)}, u32[]{:S(2)}, u32[]{:S(2)}) collective-permute-start(bf16[256,128]{1,0:T(8,128)(2,1)S(1)} %get-tuple-element.120.refs_0_), channel_id=1, source_target_pairs={{0,16},{4,20},{8,24},{12,28},{16,0},{20,4},{24,8},{28,12},{1,17},{... | collective-permute-start | bytes 196616 | tf_op jit(solution)/shard_map/ppermute | solution.py:128
  83.5 5.2 %collective-permute-start.48 = (bf16[256,128]{1,0:T(8,128)(2,1)S(1)}, bf16[256,128]{1,0:T(8,128)(2,1)S(1)}, u32[]{:S(2)}, u32[]{:S(2)}) collective-permute-start(bf16[256,128]{1,0:T(8,128)(2,1)S(1)} %get-tuple-element.120.refs_0_), channel_id=1, source_target_pairs={{0,24},{4,28},{8,16},{12,20},{16,8},{20,12},{24,0},{28,4},{1,25},{... | collective-permute-start | bytes 196616 | tf_op jit(solution)/shard_map/ppermute | solution.py:128
  85.3 5.0 %collective-permute-start.43 = (bf16[256,128]{1,0:T(8,128)(2,1)S(1)}, bf16[256,128]{1,0:T(8,128)(2,1)S(1)}, u32[]{:S(2)}, u32[]{:S(2)}) collective-permute-start(bf16[256,128]{1,0:T(8,128)(2,1)S(1)} %get-tuple-element.120.refs_0_), channel_id=1, source_target_pairs={{0,4},{4,0},{8,12},{12,8},{16,20},{20,16},{24,28},{28,24},{1,5},{5... | collective-permute-start | bytes 196616 | tf_op jit(solution)/shard_map/ppermute | solution.py:128
  88.7 7.9 %collective-permute-start.64 = (f32[32,256]{1,0:T(8,128)S(1)}, f32[32,256]{1,0:T(8,128)S(1)}, u32[]{:S(2)}, u32[]{:S(2)}) collective-permute-start(f32[32,256]{1,0:T(8,128)S(1)} %get-tuple-element.142), channel_id=1, source_target_pairs={{0,8},{4,12},{8,0},{12,4},{16,24},{20,28},{24,16},{28,20},{1,9},{5... | collective-permute-start | bytes 98312 | tf_op jit(solution)/shard_map/ppermute | solution.py:128
  91.2 10.4 %collective-permute-start.50 = (bf16[256,128]{1,0:T(8,128)(2,1)S(1)}, bf16[256,128]{1,0:T(8,128)(2,1)S(1)}, u32[]{:S(2)}, u32[]{:S(2)}) collective-permute-start(bf16[256,128]{1,0:T(8,128)(2,1)S(1)} %get-tuple-element.122), channel_id=1, source_target_pairs={{0,1},{1,0},{2,3},{3,2},{4,5},{5,4},{6,7},{7,6},{8,9},{9,8},{10,11... | collective-permute-start | bytes 196616 | tf_op jit(solution)/shard_map/ppermute | solution.py:128
  91.2 10.4 %collective-permute-start.51 = (bf16[256,128]{1,0:T(8,128)(2,1)S(1)}, bf16[256,128]{1,0:T(8,128)(2,1)S(1)}, u32[]{:S(2)}, u32[]{:S(2)}) collective-permute-start(bf16[256,128]{1,0:T(8,128)(2,1)S(1)} %get-tuple-element.123), channel_id=1, source_target_pairs={{0,2},{1,3},{2,0},{3,1},{4,6},{5,7},{6,4},{7,5},{8,10},{9,11},{10,... | collective-permute-start | bytes 196616 | tf_op jit(solution)/shard_map/ppermute | solution.py:128
  93.4 8.2 %collective-permute-start.52 = (bf16[256,128]{1,0:T(8,128)(2,1)S(1)}, bf16[256,128]{1,0:T(8,128)(2,1)S(1)}, u32[]{:S(2)}, u32[]{:S(2)}) collective-permute-start(bf16[256,128]{1,0:T(8,128)(2,1)S(1)} %get-tuple-element.124), channel_id=1, source_target_pairs={{0,3},{1,2},{2,1},{3,0},{4,7},{5,6},{6,5},{7,4},{8,11},{9,10},{10,... | collective-permute-start | bytes 196616 | tf_op jit(solution)/shard_map/ppermute | solution.py:128
  96.6 4.8 %collective-permute-start.66 = (f32[32,256]{1,0:T(8,128)S(1)}, f32[32,256]{1,0:T(8,128)S(1)}, u32[]{:S(2)}, u32[]{:S(2)}) collective-permute-start(f32[32,256]{1,0:T(8,128)S(1)} %get-tuple-element.144), channel_id=1, source_target_pairs={{0,24},{4,28},{8,16},{12,20},{16,8},{20,12},{24,0},{28,4},{1,25},{... | collective-permute-start | bytes 98312 | tf_op jit(solution)/shard_map/ppermute | solution.py:128
  101.5 11.0 %collective-permute-start.67 = (f32[32,256]{1,0:T(8,128)S(1)}, f32[32,256]{1,0:T(8,128)S(1)}, u32[]{:S(2)}, u32[]{:S(2)}) collective-permute-start(f32[32,256]{1,0:T(8,128)S(1)} %shard_map.137.refs_0_), channel_id=1, source_target_pairs={{0,1},{1,0},{2,3},{3,2},{4,5},{5,4},{6,7},{7,6},{8,9},{9,8},{10,11... | collective-permute-start | bytes 98312 | tf_op jit(solution)/shard_map/ppermute | solution.py:128
  107.0 26.0 %collective-permute-start.53 = (f32[256,128]{1,0:T(8,128)}, f32[256,128]{1,0:T(8,128)S(1)}, u32[]{:S(2)}, u32[]{:S(2)}) collective-permute-start(f32[256,128]{1,0:T(8,128)} %get-tuple-element.126), channel_id=1, source_target_pairs={{0,1},{1,0},{2,3},{3,2},{4,5},{5,4},{6,7},{7,6},{8,9},{9,8},{10,11... | collective-permute-start | bytes 393224 | tf_op jit(solution)/shard_map/ppermute | solution.py:128
  109.1 24.4 %collective-permute-start.54 = (f32[256,128]{1,0:T(8,128)}, f32[256,128]{1,0:T(8,128)S(1)}, u32[]{:S(2)}, u32[]{:S(2)}) collective-permute-start(f32[256,128]{1,0:T(8,128)} %get-tuple-element.127), channel_id=1, source_target_pairs={{0,2},{1,3},{2,0},{3,1},{4,6},{5,7},{6,4},{7,5},{8,10},{9,11},{10,... | collective-permute-start | bytes 393224 | tf_op jit(solution)/shard_map/ppermute | solution.py:128
  109.1 24.5 %collective-permute-start.55 = (f32[256,128]{1,0:T(8,128)}, f32[256,128]{1,0:T(8,128)S(1)}, u32[]{:S(2)}, u32[]{:S(2)}) collective-permute-start(f32[256,128]{1,0:T(8,128)} %get-tuple-element.128), channel_id=1, source_target_pairs={{0,3},{1,2},{2,1},{3,0},{4,7},{5,6},{6,5},{7,4},{8,11},{9,10},{10,... | collective-permute-start | bytes 393224 | tf_op jit(solution)/shard_map/ppermute | solution.py:128
  111.5 12.6 %collective-permute-start.68 = (f32[32,256]{1,0:T(8,128)S(1)}, f32[32,256]{1,0:T(8,128)S(1)}, u32[]{:S(2)}, u32[]{:S(2)}) collective-permute-start(f32[32,256]{1,0:T(8,128)S(1)} %shard_map.137.refs_0_), channel_id=1, source_target_pairs={{0,2},{1,3},{2,0},{3,1},{4,6},{5,7},{6,4},{7,5},{8,10},{9,11},{10,... | collective-permute-start | bytes 98312 | tf_op jit(solution)/shard_map/ppermute | solution.py:128
  112.4 11.7 %collective-permute-start.69 = (f32[32,256]{1,0:T(8,128)S(1)}, f32[32,256]{1,0:T(8,128)S(1)}, u32[]{:S(2)}, u32[]{:S(2)}) collective-permute-start(f32[32,256]{1,0:T(8,128)S(1)} %shard_map.137.refs_0_), channel_id=1, source_target_pairs={{0,3},{1,2},{2,1},{3,0},{4,7},{5,6},{6,5},{7,4},{8,11},{9,10},{10,... | collective-permute-start | bytes 98312 | tf_op jit(solution)/shard_map/ppermute | solution.py:128
  128.1 4.8 %collective-permute-start.75 = (f32[32,256]{1,0:T(8,128)S(1)}, f32[32,256]{1,0:T(8,128)S(1)}, u32[]{:S(2)}, u32[]{:S(2)}) collective-permute-start(f32[32,256]{1,0:T(8,128)S(1)} %shard_map.138.refs_0_), channel_id=1, source_target_pairs={{0,24},{4,28},{8,16},{12,20},{16,8},{20,12},{24,0},{28,4},{1,25},{... | collective-permute-start | bytes 98312 | tf_op jit(solution)/shard_map/ppermute | solution.py:128
  129.6 6.1 %collective-permute-start.70 = (f32[32,256]{1,0:T(8,128)S(1)}, f32[32,256]{1,0:T(8,128)S(1)}, u32[]{:S(2)}, u32[]{:S(2)}) collective-permute-start(f32[32,256]{1,0:T(8,128)S(1)} %shard_map.138.refs_0_), channel_id=1, source_target_pairs={{0,4},{4,0},{8,12},{12,8},{16,20},{20,16},{24,28},{28,24},{1,5},{5... | collective-permute-start | bytes 98312 | tf_op jit(solution)/shard_map/ppermute | solution.py:128
  133.5 23.3 %collective-permute-start.40 = (f32[64,128]{1,0:T(8,128)S(1)}, f32[64,128]{1,0:T(8,128)S(1)}, u32[]{:S(2)}, u32[]{:S(2)}) collective-permute-start(f32[64,128]{1,0:T(8,128)S(1)} %get-tuple-element.116), channel_id=1, source_target_pairs={{0,1},{1,0},{2,3},{3,2},{4,5},{5,4},{6,7},{7,6},{8,9},{9,8},{10,11... | collective-permute-start | bytes 98312 | tf_op jit(solution)/shard_map/ppermute | solution.py:128
  135.7 6.1 %collective-permute-start.61 = (f32[256,128]{1,0:T(8,128)S(1)}, f32[256,128]{1,0:T(8,128)S(1)}, u32[]{:S(2)}, u32[]{:S(2)}) collective-permute-start(f32[256,128]{1,0:T(8,128)S(1)} %get-tuple-element.136), channel_id=1, source_target_pairs={{0,4},{4,0},{8,12},{12,8},{16,20},{20,16},{24,28},{28,24},{1,5},{5... | collective-permute-start | bytes 393224 | tf_op jit(solution)/shard_map/ppermute | solution.py:128
  136.0 7.5 %collective-permute-start.59 = (f32[256,128]{1,0:T(8,128)S(1)}, f32[256,128]{1,0:T(8,128)S(1)}, u32[]{:S(2)}, u32[]{:S(2)}) collective-permute-start(f32[256,128]{1,0:T(8,128)S(1)} %get-tuple-element.134), channel_id=1, source_target_pairs={{0,4},{4,0},{8,12},{12,8},{16,20},{20,16},{24,28},{28,24},{1,5},{5... | collective-permute-start | bytes 393224 | tf_op jit(solution)/shard_map/ppermute | solution.py:128
  136.3 8.1 %collective-permute-start.57 = (f32[256,128]{1,0:T(8,128)S(1)}, f32[256,128]{1,0:T(8,128)S(1)}, u32[]{:S(2)}, u32[]{:S(2)}) collective-permute-start(f32[256,128]{1,0:T(8,128)S(1)} %get-tuple-element.132), channel_id=1, source_target_pairs={{0,4},{4,0},{8,12},{12,8},{16,20},{20,16},{24,28},{28,24},{1,5},{5... | collective-permute-start | bytes 393224 | tf_op jit(solution)/shard_map/ppermute | solution.py:128
  141.4 8.6 %collective-permute-start.56 = (f32[256,128]{1,0:T(8,128)S(1)}, f32[256,128]{1,0:T(8,128)S(1)}, u32[]{:S(2)}, u32[]{:S(2)}) collective-permute-start(f32[256,128]{1,0:T(8,128)S(1)} %get-tuple-element.130), channel_id=1, source_target_pairs={{0,4},{4,0},{8,12},{12,8},{16,20},{20,16},{24,28},{28,24},{1,5},{5... | collective-permute-start | bytes 393224 | tf_op jit(solution)/shard_map/ppermute | solution.py:128
  141.9 9.3 %collective-permute-start.62 = (f32[256,128]{1,0:T(8,128)S(1)}, f32[256,128]{1,0:T(8,128)S(1)}, u32[]{:S(2)}, u32[]{:S(2)}) collective-permute-start(f32[256,128]{1,0:T(8,128)S(1)} %add.23), channel_id=1, source_target_pairs={{0,24},{4,28},{8,16},{12,20},{16,8},{20,12},{24,0},{28,4},{1,25},{... | collective-permute-start | bytes 393224 | tf_op jit(solution)/shard_map/ppermute | solution.py:128
  143.5 10.1 %collective-permute-start.60 = (f32[256,128]{1,0:T(8,128)S(1)}, f32[256,128]{1,0:T(8,128)S(1)}, u32[]{:S(2)}, u32[]{:S(2)}) collective-permute-start(f32[256,128]{1,0:T(8,128)S(1)} %add.22), channel_id=1, source_target_pairs={{0,16},{4,20},{8,24},{12,28},{16,0},{20,4},{24,8},{28,12},{1,17},{... | collective-permute-start | bytes 393224 | tf_op jit(solution)/shard_map/ppermute | solution.py:128
  144.5 9.1 %collective-permute-start.58 = (f32[256,128]{1,0:T(8,128)S(1)}, f32[256,128]{1,0:T(8,128)S(1)}, u32[]{:S(2)}, u32[]{:S(2)}) collective-permute-start(f32[256,128]{1,0:T(8,128)S(1)} %add.21), channel_id=1, source_target_pairs={{0,8},{4,12},{8,0},{12,4},{16,24},{20,28},{24,16},{28,20},{1,9},{5... | collective-permute-start | bytes 393224 | tf_op jit(solution)/shard_map/ppermute | solution.py:128
  150.1 9.2 %collective-permute-start.41 = (f32[64,128]{1,0:T(8,128)S(1)}, f32[64,128]{1,0:T(8,128)S(1)}, u32[]{:S(2)}, u32[]{:S(2)}) collective-permute-start(f32[64,128]{1,0:T(8,128)S(1)} %get-tuple-element.117), channel_id=1, source_target_pairs={{0,2},{1,3},{2,0},{3,1},{4,6},{5,7},{6,4},{7,5},{8,10},{9,11},{10,... | collective-permute-start | bytes 98312 | tf_op jit(solution)/shard_map/ppermute | solution.py:128
  151.1 8.1 %collective-permute-start.42 = (f32[64,128]{1,0:T(8,128)S(1)}, f32[64,128]{1,0:T(8,128)S(1)}, u32[]{:S(2)}, u32[]{:S(2)}) collective-permute-start(f32[64,128]{1,0:T(8,128)S(1)} %get-tuple-element.118), channel_id=1, source_target_pairs={{0,3},{1,2},{2,1},{3,0},{4,7},{5,6},{6,5},{7,4},{8,11},{9,10},{10,... | collective-permute-start | bytes 98312 | tf_op jit(solution)/shard_map/ppermute | solution.py:128
  154.8 5.2 %collective-permute-start.77 = (f32[64,128]{1,0:T(8,128)S(1)}, f32[64,128]{1,0:T(8,128)S(1)}, u32[]{:S(2)}, u32[]{:S(2)}) collective-permute-start(f32[64,128]{1,0:T(8,128)S(1)} %get-tuple-element.148), channel_id=1, source_target_pairs={{0,1},{1,0},{2,3},{3,2},{4,5},{5,4},{6,7},{7,6},{8,9},{9,8},{10,11... | collective-permute-start | bytes 98312 | tf_op jit(solution)/shard_map/ppermute | solution.py:128
  154.9 5.2 %collective-permute-start.78 = (f32[64,128]{1,0:T(8,128)S(1)}, f32[64,128]{1,0:T(8,128)S(1)}, u32[]{:S(2)}, u32[]{:S(2)}) collective-permute-start(f32[64,128]{1,0:T(8,128)S(1)} %get-tuple-element.149), channel_id=1, source_target_pairs={{0,2},{1,3},{2,0},{3,1},{4,6},{5,7},{6,4},{7,5},{8,10},{9,11},{10,... | collective-permute-start | bytes 98312 | tf_op jit(solution)/shard_map/ppermute | solution.py:128
  156.8 5.7 %collective-permute-start.79 = (f32[64,128]{1,0:T(8,128)S(1)}, f32[64,128]{1,0:T(8,128)S(1)}, u32[]{:S(2)}, u32[]{:S(2)}) collective-permute-start(f32[64,128]{1,0:T(8,128)S(1)} %get-tuple-element.150), channel_id=1, source_target_pairs={{0,3},{1,2},{2,1},{3,0},{4,7},{5,6},{6,5},{7,4},{8,11},{9,10},{10,... | collective-permute-start | bytes 98312 | tf_op jit(solution)/shard_map/ppermute | solution.py:128
  (33 other events, 112.3 us)
where the time goes:
time: 164 us; the launch traced here: 163 us
  starting transfers between devices  75.5 us (46%)
  waiting for transfers between devices  41.2 us (25%)
  Pallas kernels  35.1 us (21%)
  local copies, waits for them, and re-layouts  10.2 us (6%)
    ppermute x80, starting transfers between devices, swap(): return lax.ppermute(x, axis, [(i, i ^ mask) for i in range(size)])  75.5 us
    ppermute x80, waiting for transfers between devices, swap(): return lax.ppermute(x, axis, [(i, i ^ mask) for i in range(size)])  41.2 us
    pallas_call x23, Pallas kernels, kernel_call(): pl.pallas_call(kernel, out_shape=tuple(out_shape), in_specs=[spec] * len(...  25.4 us
    unnamed x36, local copies, waits for them, and re-layouts  10.2 us
    pallas_call x2, Pallas kernels, tile_sums(): pl.pallas_call(functools.partial(tile_kernel, forward, count), out_shape=...  9.61 us
  transfers between devices with their start and end apart: 80, of which 18 were waited for; matrix products, arithmetic and copies ran while one was open for 1% of the time, Pallas kernels for 20%

commit v1 on v0

--- a/solution.py
+++ b/solution.py
@@ -71,7 +71,7 @@
     wide = lax.axis_index("wide")
     for r, piece in enumerate(pieces):
         place = wide ^ r
-        start = (place % 2) * (rank // 2) + (place // 2) * height
+        start = (place % 2) * (rank // 2) + (place // 2 % 2) * height
         work_ref[pl.ds(pl.multiple_of(start, height), height), :] = piece[...]
     time = time_ref[...]
     times = lax.dot_general(
@@ -147,8 +147,8 @@
     count = lax.axis_size("narrow")
     for d in range(count):
         tile = wide * count + (narrow ^ d)
-        user = user_ref[coords_ref[tile, 0]] ^ wide
-        item = item_ref[coords_ref[tile, 1]] ^ wide
+        user = user_ref[coords_ref[0, tile]] ^ wide
+        item = item_ref[coords_ref[1, tile]] ^ wide
         table_ref[d : d + 1, :] = jnp.full((1, 128), user, jnp.int32)
         table_ref[count + d : count + d + 1, :] = jnp.full((1, 128), item, jnp.int32)
 
@@ -157,118 +157,82 @@
     count = lax.axis_size("narrow")
     (table,) = kernel_call(
         positions_kernel, [shape((2 * count, 128), jnp.int32)],
-        tile_coords, user_owner, item_owner, smem=True,
+        tile_coords.T, user_owner, item_owner, smem=True,
     )
     return table[:count], table[count:]
 
 
-def start_kernel(factor_ref, low_ref, *outputs):
-    low_ref[...] = factor_ref[...].astype(low_ref.dtype)
-    split_kernel(len(outputs), factor_ref, *outputs)
-
-
-def start(factor):
-    count = lax.axis_size("narrow")
-    height, rows = factor.shape
-    out = [shape(factor.shape, jnp.bfloat16)] + [shape((height, rows // count))] * count
-    low, *pieces = kernel_call(start_kernel, out, factor)
-    return low, pieces
-
-
-def split_kernel(count, *refs):
-    inputs, outputs = refs[: -count], refs[-count:]
+def start_kernel(stack_ref, *outputs):
     width = outputs[0].shape[1]
-    height = inputs[0].shape[0]
 
     def body(v):
         for d, out in enumerate(outputs):
-            lanes = slice((v ^ d) * width, ((v ^ d) + 1) * width)
-            first = inputs[0][:, lanes]
-            if len(inputs) > 1:
-                first = first + inputs[1][:, lanes]
-            out[:height, :] = first
-            for k in range(1, len(inputs)):
-                out[k * height : (k + 1) * height, :] = inputs[k][:, lanes]
+            out[...] = stack_ref[:, (v ^ d) * width : ((v ^ d) + 1) * width]
 
     for_each_position(body)
 
 
-def split(*arrays):
-    count = lax.axis_size("narrow")
-    height, rows = arrays[0].shape
-    out = [shape((len(arrays) * height, rows // count))] * count
-    return kernel_call(functools.partial(split_kernel, count), out, *arrays)
-
-
-def halves(gram, give_ref, keep_ref):
-    half = keep_ref.shape[0]
+def start(item_factor, item_dual, user_factor, user_dual):
+    count = lax.axis_size("narrow")
+    stack = jnp.concatenate([item_factor, user_factor + user_dual, user_dual, item_dual])
+    height, rows = stack.shape
+    return kernel_call(start_kernel, [shape((height, rows // count))] * count, stack)
+
+
+def gram_parts(rows, far_ref, near_ref):
+    gram = lax.dot_general(
+        rows, rows, (((1,), (1,)), ((), ())), precision=HIGHEST, preferred_element_type=jnp.float32
+    )
+    half = near_ref.shape[0]
     for core in range(2):
 
         @pl.when(lax.axis_index("wide") % 2 == core)
         def _(core=core):
-            keep_ref[...] = gram[core * half : (core + 1) * half]
-            give_ref[...] = gram[(1 - core) * half : (2 - core) * half]
-
-
-def gram_of(rows):
-    return lax.dot_general(
-        rows, rows, (((1,), (1,)), ((), ())), precision=HIGHEST, preferred_element_type=jnp.float32
-    )
-
-
-def gram_kernel(*refs):
-    pieces, (rows_ref, give_ref, keep_ref) = refs[:-3], refs[-3:]
-    height = pieces[0].shape[0]
+            near_ref[...] = gram[core * half : (core + 1) * half]
+            far_ref[...] = gram[(1 - core) * half : (2 - core) * half]
+
+
+def gram_kernel(count, *refs):
+    pieces, (factor_ref, far_ref, near_ref) = refs[:count], refs[count:]
+    height = pieces[0].shape[0] // 4
     for d, piece in enumerate(pieces):
-        rows_ref[rows_of(d, height), :] = piece[...]
-    halves(gram_of(rows_ref[...]), give_ref, keep_ref)
-
-
-def assemble_kernel(*refs):
-    factor_ref, pieces, outputs = refs[0], refs[1:-4], refs[-4:]
-    height = pieces[0].shape[0] // 3
+        factor_ref[rows_of(d, height), :] = piece[:height]
+    gram_parts(factor_ref[...], far_ref, near_ref)
+
+
+def assemble_kernel(count, *refs):
+    factor_ref, pieces, outputs = refs[0], refs[1 : count + 1], refs[count + 1 :]
+    height = pieces[0].shape[0] // 4
     for d, piece in enumerate(pieces):
         rows = rows_of(d, height)
-        outputs[0][rows, :] = piece[:height]
-        outputs[1][rows, :] = piece[height : 2 * height]
-        outputs[3][rows, :] = piece[2 * height :]
+        outputs[0][rows, :] = piece[height : 2 * height]
+        outputs[1][rows, :] = piece[2 * height : 3 * height]
+        outputs[3][rows, :] = piece[3 * height :]
     outputs[2][...] = factor_ref[...] + outputs[3][...]
 
 
-def chip_sum_kernel(keep_ref, got_ref, *refs):
-    outputs, total_ref = refs[:-1], refs[-1]
-    total_ref[...] = keep_ref[...] + got_ref[...]
-    height = outputs[0].shape[0]
-    chip = lax.axis_index("wide") // 2
-    for m, out in enumerate(outputs):
-        out[...] = total_ref[pl.ds(pl.multiple_of((chip ^ m) * height, height), height), :]
-
-
-def sum_kernel(*refs):
-    total = refs[0][...]
-    for x in refs[1:-1]:
-        total = total + x[...]
-    refs[-1][...] = total
-
-
-def add_up(pieces):
-    (total,) = kernel_call(sum_kernel, [shape(pieces[0].shape)], *pieces)
-    return total
-
-
-def sum_everywhere(give, keep):
-    chips = lax.axis_size("wide") // 2
-    half, rank = keep.shape
-    got = swap(give, "wide", 1)
-    pieces = kernel_call(
-        chip_sum_kernel, [shape((half // chips, rank))] * chips, keep, got,
+def chip_sum_kernel(near_ref, got_ref, far_out, near_out, total_ref):
+    total_ref[...] = near_ref[...] + got_ref[...]
+    height = near_out.shape[0]
+    side = (lax.axis_index("wide") // 2) % 2
+    near_out[...] = total_ref[pl.ds(pl.multiple_of(side * height, height), height), :]
+    far_out[...] = total_ref[pl.ds(pl.multiple_of((1 - side) * height, height), height), :]
+
+
+def sum_everywhere(far, near):
+    half, rank = near.shape
+    got = swap(far, "wide", 1)
+    far, near = kernel_call(
+        chip_sum_kernel, [shape((half // 2, rank))] * 2, near, got,
         scratch=[pltpu.VMEM((half, rank), jnp.float32)],
     )
-    pieces = [pieces[0]] + [swap(pieces[m], "wide", 2 * m) for m in range(1, chips)]
-    mine = add_up(pieces)
-    mine = add_up(swaps([mine] * lax.axis_size("narrow")))
-    pieces = [mine] + [swap(mine, "wide", 2 * m) for m in range(1, chips)]
-    return [x for a in pieces for x in (a, swap(a, "wide", 1))]
+    total = near + swap(far, "wide", 2)
+    for axis, mask in (("wide", 4), ("narrow", 1)):
+        while mask < lax.axis_size(axis):
+            total = total + swap(total, axis, mask)
+            mask *= 2
+    parts = [total, swap(total, "wide", 2)]
+    return [x for part in parts for x in (part, swap(part, "wide", 1))]
 
 
 def pick_kernel(count, table_ref, *refs):
@@ -289,32 +253,24 @@
     count = lax.axis_size("narrow")
     picked = kernel_call(
         functools.partial(pick_kernel, count), [shape(lowered.shape, lowered.dtype)] * count,
-        table, *blocks,
+        table, *blocks, flops=5_000_000_000,
     )
     return swaps(picked)
 
 
 def tile_kernel(forward, count, activity_ref, time_ref, *refs):
-    pieces, outputs = refs[:count], refs[count : 2 * count]
-    tile_ref, stage_ref, sums_ref, sems = refs[2 * count :]
-    steps = activity_ref.shape[1]
-    copies = [
-        pltpu.make_async_copy(activity_ref.at[0, k], tile_ref.at[k], sems.at[k])
-        for k in range(steps)
-    ]
-    for copy in copies:
-        copy.start()
+    pieces, outputs, (stage_ref, sums_ref) = refs[:count], refs[count : 2 * count], refs[2 * count :]
     me = lax.axis_index("narrow")
     for d, piece in enumerate(pieces):
         stage_ref[me ^ d] = piece[...]
     low = jnp.concatenate([stage_ref[q] for q in range(count)], axis=0 if forward else 1)
     low = low.astype(jnp.float32)
+    times = time_ref[...].T
     total = None
-    for k in range(steps):
-        khatri = (low * time_ref[:, k : k + 1]).astype(jnp.bfloat16)
+    for k in range(activity_ref.shape[1]):
+        khatri = (low * times[:, k : k + 1]).astype(jnp.bfloat16)
         dims = (((1,), (1 if forward else 0,)), ((), ()))
-        copies[k].wait()
-        term = lax.dot_general(khatri, tile_ref[k], dims, preferred_element_type=jnp.float32)
+        term = lax.dot_general(khatri, activity_ref[0, k], dims, preferred_element_type=jnp.float32)
         total = term if total is None else total + term
     width = outputs[0].shape[1]
     for q in range(count):
@@ -323,29 +279,20 @@
         out[...] = sums_ref[me ^ d]
 
 
-def tile_sums(activity, pieces, time_by_rank, forward):
+def tile_sums(activity, pieces, time_factor, forward):
     count = len(pieces)
-    rank = time_by_rank.shape[0]
+    rank = time_factor.shape[1]
     _, steps, rows, cols = activity.shape
     width = (rows if forward else cols) // count
-    inside = pl.BlockSpec(memory_space=pltpu.VMEM)
-    return pl.pallas_call(
-        functools.partial(tile_kernel, forward, count),
-        out_shape=(shape((rank, width)),) * count,
-        in_specs=[pl.BlockSpec(memory_space=pl.ANY)] + [inside] * (count + 1),
-        out_specs=(inside,) * count,
-        scratch_shapes=[
-            pltpu.VMEM(activity.shape[1:], activity.dtype),
+    return kernel_call(
+        functools.partial(tile_kernel, forward, count), [shape((rank, width))] * count,
+        activity, time_factor, *pieces,
+        scratch=[
             pltpu.VMEM((count, *pieces[0].shape), jnp.bfloat16),
             pltpu.VMEM((count, rank, width), jnp.float32),
-            pltpu.SemaphoreType.DMA((steps,)),
         ],
-        compiler_params=pltpu.CompilerParams(vmem_limit_bytes=60 * 2**20),
-        cost_estimate=pl.CostEstimate(
-            flops=2_000_000_000, bytes_accessed=2 * activity.size, transcendentals=0
-        ),
-        name="tile",
-    )(activity, time_by_rank, *pieces)
+        flops=2 * rank * steps * rows * cols,
+    )
 
 
 def place_kernel(count, table_ref, *refs):
@@ -396,10 +343,10 @@
     for d in range(count):
         outputs[d][...] = value_ref[rows_of(d, height), :]
     if len(outputs) > count + 1:
-        low_ref, give_ref, keep_ref = outputs[count : count + 3]
+        low_ref, far_ref, near_ref = outputs[count : count + 3]
         fresh = jnp.maximum(value, 0.0)
         low_ref[...] = fresh.astype(low_ref.dtype)
-        halves(gram_of(fresh), give_ref, keep_ref)
+        gram_parts(fresh, far_ref, near_ref)
 
 
 def admm(terms, shifted, dual, penalty, inverse, more):
@@ -463,29 +410,30 @@
     user_dual, item_dual,
 ):
     rank = time_factor.shape[1]
-    time_by_rank = time_factor.T
-    low, item_pieces = start(item_factor)
+    count = lax.axis_size("narrow")
     user_table, item_table = positions(tile_coords, user_owner, item_owner)
 
-    item_pieces = swaps(item_pieces)
-    width = item_pieces[0].shape[1]
-    item_rows, *gram = kernel_call(
-        gram_kernel, [shape((rank, width))] + [shape((rank // 2, rank))] * 2, *item_pieces,
+    pieces = swaps(start(item_factor, item_dual, user_factor, user_dual))
+    width = pieces[0].shape[1]
+    half = shape((rank // 2, rank))
+    item_rows, far, near = kernel_call(
+        functools.partial(gram_kernel, count), [shape((rank, width)), half, half], *pieces,
         flops=12 * rank * rank * width,
     )
-    other_pieces = swaps(split(user_factor, user_dual, item_dual))
     user_shifted, udual_rows, item_shifted, idual_rows = kernel_call(
-        assemble_kernel, [shape((rank, width))] * 4, item_rows, *other_pieces
-    )
-
-    partials = tile_sums(activity, fetch_rows(low, item_table), time_by_rank, True)
+        functools.partial(assemble_kernel, count), [shape((rank, width))] * 4,
+        item_rows, *pieces,
+    )
+
+    low = item_factor.astype(jnp.bfloat16)
+    partials = tile_sums(activity, fetch_rows(low, item_table), time_factor, True)
     terms = owner_sums(partials, user_table)
-    penalty, inverse = penalty_inverse(sum_everywhere(*gram), time_factor)
-    *user_pieces, low, give, keep = admm(terms, user_shifted, udual_rows, penalty, inverse, True)
-
-    partials = tile_sums(activity, fetch_rows(low, user_table), time_by_rank, False)
+    penalty, inverse = penalty_inverse(sum_everywhere(far, near), time_factor)
+    *user_pieces, low, far, near = admm(terms, user_shifted, udual_rows, penalty, inverse, True)
+
+    partials = tile_sums(activity, fetch_rows(low, user_table), time_factor, False)
     terms = owner_sums(partials, item_table)
-    penalty, inverse = penalty_inverse(sum_everywhere(give, keep), time_factor)
+    penalty, inverse = penalty_inverse(sum_everywhere(far, near), time_factor)
     new_users, new_user_dual = to_columns(user_pieces)
     item_pieces = admm(terms, item_shifted, idual_rows, penalty, inverse, False)
     new_items, new_item_dual = to_columns(item_pieces)

time: 164 us -> 146 us (0.89)
  starting transfers between devices: 75.5 us -> 62.7 us
  local copies, waits for them, and re-layouts: 10.2 us -> 2 us
  waiting for transfers between devices: 41.2 us -> 49.2 us
  Pallas kernels: 35.1 us -> 28 us
  other arithmetic: 0.09 us -> 3.14 us
    ppermute x80 -> x65, starting transfers between devices: 75.5 us -> 62.7 us  [swap(): return lax.ppermute(x, axis, [(i, i ^ mask) for i in range(size)])]
    pallas_call x2 -> x0, Pallas kernels: 9.61 us -> none  [tile_sums(): pl.pallas_call(functools.partial(tile_kernel, forward, count), out_shape=...]
    unnamed x36 -> x10, local copies, waits for them, and re-layouts: 10.2 us -> 2 us
    ppermute x80 -> x65, waiting for transfers between devices: 41.2 us -> 49.2 us  [swap(): return lax.ppermute(x, axis, [(i, i ^ mask) for i in range(size)])]
    pallas_call x23 -> x20, Pallas kernels: 25.4 us -> 28 us  [kernel_call(): pl.pallas_call(kernel, out_shape=tuple(out_shape), in_specs=[spec] * len(...]
  transfers between devices with their start and end apart: 80 -> 65, of which waited for: 18 -> 18; matrix products, arithmetic and copies ran while one was open for 1% -> 1% of each run, Pallas kernels for 20% -> 17%
where the time goes in v1:
time: 146 us
  starting transfers between devices  62.7 us (43%)
  waiting for transfers between devices  49.2 us (34%)
  Pallas kernels  28 us (19%)
  other arithmetic  3.14 us (2%)
  local copies, waits for them, and re-layouts  2 us (1%)
    ppermute x65, starting transfers between devices, swap(): return lax.ppermute(x, axis, [(i, i ^ mask) for i in range(size)])  62.7 us
    ppermute x65, waiting for transfers between devices, swap(): return lax.ppermute(x, axis, [(i, i ^ mask) for i in range(size)])  49.2 us
    pallas_call x20, Pallas kernels, kernel_call(): pl.pallas_call(kernel, out_shape=tuple(out_shape), in_specs=[spec] * len(...  28 us
  transfers between devices with their start and end apart: 65, of which 18 were waited for; matrix products, arithmetic and copies ran while one was open for 1% of the time, Pallas kernels for 17%

profile of v1, /device:TPU:0, one launch (start us, length us, event | category | flops | bytes accessed | tf_op | source)
XLA Modules:
  0.0 146.1 jit_solution(4494636151679373703)
XLA Ops:
  0.6 1.0 bitcast_add_fusion
  1.6 1.1 pad_maximum_fusion.stack_ref
  2.8 3.1 %collective-permute-start.20 = (f32[256,128]{1,0:T(8,128)S(1)}, f32[256,128]{1,0:T(8,128)S(1)}, u32[]{:S(2)}, u32[]{:S(2)}) collective-permute-start(f32[256,128]{1,0:T(8,128)S(1)} %get-tuple-element.87), channel_id=1, source_target_pairs={{0,1},{1,0},{2,3},{3,2},{4,5},{5,4},{6,7},{7,6},{8,9},{9,8},{10,11... | collective-permute-start | bytes 393224 | tf_op jit(solution)/shard_map/ppermute | solution.py:128
  5.9 2.6 %collective-permute-start.21 = (f32[256,128]{1,0:T(8,128)S(1)}, f32[256,128]{1,0:T(8,128)S(1)}, u32[]{:S(2)}, u32[]{:S(2)}) collective-permute-start(f32[256,128]{1,0:T(8,128)S(1)} %get-tuple-element.88), channel_id=1, source_target_pairs={{0,2},{1,3},{2,0},{3,1},{4,6},{5,7},{6,4},{7,5},{8,10},{9,11},{10,... | collective-permute-start | bytes 393224 | tf_op jit(solution)/shard_map/ppermute | solution.py:128
  8.5 0.9 bitcast_convert_fusion.refs_0_
  9.4 1.6 %collective-permute-start.1 = (bf16[64,512]{1,0:T(8,128)(2,1)S(1)}, bf16[64,512]{1,0:T(8,128)(2,1)S(1)}, u32[]{:S(2)}, u32[]{:S(2)}) collective-permute-start(bf16[64,512]{1,0:T(8,128)(2,1)S(1)} %bitcast_convert_fusion.refs_0_), channel_id=1, source_target_pairs={{0,8},{4,12},{8,0},{12,4},{16,24},{20,28},{24,16},{28,20},{1,9},{5... | collective-permute-start | bytes 196616 | tf_op jit(solution)/shard_map/ppermute | solution.py:128
  10.9 1.5 %collective-permute-start.3 = (bf16[64,512]{1,0:T(8,128)(2,1)S(1)}, bf16[64,512]{1,0:T(8,128)(2,1)S(1)}, u32[]{:S(2)}, u32[]{:S(2)}) collective-permute-start(bf16[64,512]{1,0:T(8,128)(2,1)S(1)} %bitcast_convert_fusion.refs_0_), channel_id=1, source_target_pairs={{0,16},{4,20},{8,24},{12,28},{16,0},{20,4},{24,8},{28,12},{1,17},{... | collective-permute-start | bytes 196616 | tf_op jit(solution)/shard_map/ppermute | solution.py:128
  12.9 0.7 copy-done.2
  13.6 0.7 copy-done.3
  14.3 0.7 copy-done.4
  16.1 1.5 %collective-permute-done.5.refs_6_ = bf16[64,512]{1,0:T(8,128)(2,1)S(1)} collective-permute-done((bf16[64,512]{1,0:T(8,128)(2,1)S(1)}, bf16[64,512]{1,0:T(8,128)(2,1)S(1)}, u32[]{:S(2)}, u32[]{:S(2)}) %collective-permute-start.5) | collective-permute-done | bytes 65568 | tf_op jit(solution)/shard_map/ppermute | solution.py:128
  18.2 5.2 %collective-permute-done.22.refs_3_.refs_4_ = f32[256,128]{1,0:T(8,128)S(1)} collective-permute-done((f32[256,128]{1,0:T(8,128)S(1)}, f32[256,128]{1,0:T(8,128)S(1)}, u32[]{:S(2)}, u32[]{:S(2)}) %collective-permute-start.22) | collective-permute-done | bytes 131104 | tf_op jit(solution)/shard_map/ppermute | solution.py:128
  24.1 1.1 collective-permute-done.23.got_ref
  25.3 1.6 %collective-permute-start.24 = (f32[64,256]{1,0:T(8,128)S(1)}, f32[64,256]{1,0:T(8,128)S(1)}, u32[]{:S(2)}, u32[]{:S(2)}) collective-permute-start(f32[64,256]{1,0:T(8,128)S(1)} %get-tuple-element.96), channel_id=1, source_target_pairs={{0,8},{4,12},{8,0},{12,4},{16,24},{20,28},{24,16},{28,20},{1,9},{5... | collective-permute-start | bytes 196616 | tf_op jit(solution)/shard_map/ppermute | solution.py:128
  26.8 1.4 collective-permute-start.7
  28.2 3.0 %collective-permute-start.9 = (bf16[64,512]{1,0:T(8,128)(2,1)S(1)}, bf16[64,512]{1,0:T(8,128)(2,1)S(1)}, u32[]{:S(2)}, u32[]{:S(2)}) collective-permute-start(bf16[64,512]{1,0:T(8,128)(2,1)S(1)} %get-tuple-element.73), channel_id=1, source_target_pairs={{0,3},{1,2},{2,1},{3,0},{4,7},{5,6},{6,5},{7,4},{8,11},{9,10},{10,... | collective-permute-start | bytes 196616 | tf_op jit(solution)/shard_map/ppermute | solution.py:128
  31.2 1.6 %collective-permute-start.25 = (f32[64,256]{1,0:T(8,128)S(1)}, f32[64,256]{1,0:T(8,128)S(1)}, u32[]{:S(2)}, u32[]{:S(2)}) collective-permute-start(f32[64,256]{1,0:T(8,128)S(1)} %add.49), channel_id=1, source_target_pairs={{0,16},{4,20},{8,24},{12,28},{16,0},{20,4},{24,8},{28,12},{1,17},{... | collective-permute-start | bytes 196616 | tf_op jit(solution)/shard_map/ppermute | solution.py:128
  32.8 3.3 %collective-permute-done.8.refs_2_ = bf16[64,512]{1,0:T(8,128)(2,1)S(1)} collective-permute-done((bf16[64,512]{1,0:T(8,128)(2,1)S(1)}, bf16[64,512]{1,0:T(8,128)(2,1)S(1)}, u32[]{:S(2)}, u32[]{:S(2)}) %collective-permute-start.8) | collective-permute-done | bytes 65568 | tf_op jit(solution)/shard_map/ppermute | solution.py:128
  36.1 1.6 %shard_map.122 = (f32[256,128]{1,0:T(8,128)S(1)}, f32[256,128]{1,0:T(8,128)S(1)}, f32[256,128]{1,0:T(8,128)S(1)}, f32[256,128]{1,0:T(8,128)S(1)}) custom-call(bf16[1,8,512,512]{3,2,1,0:T(8,128)(2,1)S(1)} %copy-done, f32[8,256]{1,0:T(8,128)S(1)} %copy-done.1, bf16[64,512]{1,0:T(8,128)(2,1)S(1)} %get-tuple-element.70.refs_0_, ...), custom_call_target="tpu_custom_call" | custom-call | flops 1073741824 | bytes 4988928 | tf_op jit(solution)/shard_map/pallas_call | solution.py:111
  37.6 1.4 collective-permute-start.10
  39.1 0.7 collective-permute-start.11
  39.8 2.3 %collective-permute-start.12 = (f32[256,128]{1,0:T(8,128)S(1)}, f32[256,128]{1,0:T(8,128)S(1)}, u32[]{:S(2)}, u32[]{:S(2)}) collective-permute-start(f32[256,128]{1,0:T(8,128)S(1)} %get-tuple-element.77), channel_id=1, source_target_pairs={{0,3},{1,2},{2,1},{3,0},{4,7},{5,6},{6,5},{7,4},{8,11},{9,10},{10,... | collective-permute-start | bytes 393224 | tf_op jit(solution)/shard_map/ppermute | solution.py:128
  42.6 5.9 %collective-permute-done.26 = f32[64,256]{1,0:T(8,128)S(1)} collective-permute-done((f32[64,256]{1,0:T(8,128)S(1)}, f32[64,256]{1,0:T(8,128)S(1)}, u32[]{:S(2)}, u32[]{:S(2)}) %collective-permute-start.26) | collective-permute-done | bytes 65568 | tf_op jit(solution)/shard_map/ppermute | solution.py:128
  48.5 2.1 %collective-permute-start.27 = (f32[64,256]{1,0:T(8,128)S(1)}, f32[64,256]{1,0:T(8,128)S(1)}, u32[]{:S(2)}, u32[]{:S(2)}) collective-permute-start(f32[64,256]{1,0:T(8,128)S(1)} %add.51), channel_id=1, source_target_pairs={{0,2},{1,3},{2,0},{3,1},{4,6},{5,7},{6,4},{7,5},{8,10},{9,11},{10,... | collective-permute-start | bytes 196616 | tf_op jit(solution)/shard_map/ppermute | solution.py:128
  51.8 3.1 %collective-permute-done.27 = f32[64,256]{1,0:T(8,128)S(1)} collective-permute-done((f32[64,256]{1,0:T(8,128)S(1)}, f32[64,256]{1,0:T(8,128)S(1)}, u32[]{:S(2)}, u32[]{:S(2)}) %collective-permute-start.27) | collective-permute-done | bytes 65568 | tf_op jit(solution)/shard_map/ppermute | solution.py:128
  54.9 0.6 collective-permute-start.29
  55.6 3.7 %collective-permute-done.29.refs_2_ = f32[64,256]{1,0:T(8,128)S(1)} collective-permute-done((f32[64,256]{1,0:T(8,128)S(1)}, f32[64,256]{1,0:T(8,128)S(1)}, u32[]{:S(2)}, u32[]{:S(2)}) %collective-permute-start.29) | collective-permute-done | bytes 65568 | tf_op jit(solution)/shard_map/ppermute | solution.py:128
  60.6 1.6 %collective-permute-start.17 = (f32[256,128]{1,0:T(8,128)S(1)}, f32[256,128]{1,0:T(8,128)S(1)}, u32[]{:S(2)}, u32[]{:S(2)}) collective-permute-start(f32[256,128]{1,0:T(8,128)S(1)} %add.46), channel_id=1, source_target_pairs={{0,16},{4,20},{8,24},{12,28},{16,0},{20,4},{24,8},{28,12},{1,17},{... | collective-permute-start | bytes 393224 | tf_op jit(solution)/shard_map/ppermute | solution.py:128
  62.2 1.5 %collective-permute-start.19 = (f32[256,128]{1,0:T(8,128)S(1)}, f32[256,128]{1,0:T(8,128)S(1)}, u32[]{:S(2)}, u32[]{:S(2)}) collective-permute-start(f32[256,128]{1,0:T(8,128)S(1)} %add.47), channel_id=1, source_target_pairs={{0,24},{4,28},{8,16},{12,20},{16,8},{20,12},{24,0},{28,4},{1,25},{... | collective-permute-start | bytes 393224 | tf_op jit(solution)/shard_map/ppermute | solution.py:128
  63.7 4.9 %shard_map.128 = (f32[256,256]{1,0:T(8,128)S(1)}, f32[1,128]{1,0:T(1,128)S(1)}) custom-call(f32[8,256]{1,0:T(8,128)S(1)} %copy-done.1, f32[64,256]{1,0:T(8,128)S(1)} %add.52.refs_0_, f32[64,256]{1,0:T(8,128)S(1)} %collective-permute-done.28.refs_1_, f32[64,256]{1,0:T(8,128)S(1)} %collective-permute-done.29.refs_2_, f32[64,256]{1,0:T(8,128)S(1)} %collective-permute-done.30.refs_3_), custom_call_target="tpu_custom_call" | custom-call | flops 6000000000 | bytes 532992 | tf_op jit(solution)/shard_map/pallas_call | solution.py:111
  68.6 4.2 %shard_map.129.refs_8_ = f32[256,256]{1,0:T(8,128)S(1)} custom-call(f32[256,256]{1,0:T(8,128)S(1)} %get-tuple-element.98.half_ref), custom_call_target="tpu_custom_call" | custom-call | flops 6000000000 | bytes 524288 | tf_op jit(solution)/shard_map/pallas_call | solution.py:111
  72.9 1.6 %shard_map.130 = (f32[64,128]{1,0:T(8,128)S(1)}, f32[64,128]{1,0:T(8,128)S(1)}, f32[64,128]{1,0:T(8,128)S(1)}, f32[64,128]{1,0:T(8,128)S(1)}, bf16[256,128]{1,0:...) custom-call(f32[256,128]{1,0:T(8,128)S(1)} %get-tuple-element.78.refs_0_, ...), custom_call_target="tpu_custom_call" | custom-call | flops 201326592 | bytes 1638912 | tf_op jit(solution)/shard_map/pallas_call | solution.py:111
  74.5 0.6 collective-permute-start.35
  75.2 1.5 %collective-permute-start.37 = (bf16[256,128]{1,0:T(8,128)(2,1)S(1)}, bf16[256,128]{1,0:T(8,128)(2,1)S(1)}, u32[]{:S(2)}, u32[]{:S(2)}) collective-permute-start(bf16[256,128]{1,0:T(8,128)(2,1)S(1)} %get-tuple-element.104.refs_0_), channel_id=1, source_target_pairs={{0,16},{4,20},{8,24},{12,28},{16,0},{20,4},{24,8},{28,12},{1,17},{... | collective-permute-start | bytes 196616 | tf_op jit(solution)/shard_map/ppermute | solution.py:128
  76.7 1.4 collective-permute-start.39
  78.1 1.2 collective-permute-done.35.refs_2_
  79.3 0.9 collective-permute-done.37.refs_4_
  80.1 1.7 %collective-permute-done.39.refs_6_ = bf16[256,128]{1,0:T(8,128)(2,1)S(1)} collective-permute-done((bf16[256,128]{1,0:T(8,128)(2,1)S(1)}, bf16[256,128]{1,0:T(8,128)(2,1)S(1)}, u32[]{:S(2)}, u32[]{:S(2)}) %collective-permute-start.39) | collective-permute-done | bytes 65568 | tf_op jit(solution)/shard_map/ppermute | solution.py:128
  82.4 0.7 collective-permute-done.40.refs_7_
  83.4 1.6 %collective-permute-start.55 = (f32[64,256]{1,0:T(8,128)S(1)}, f32[64,256]{1,0:T(8,128)S(1)}, u32[]{:S(2)}, u32[]{:S(2)}) collective-permute-start(f32[64,256]{1,0:T(8,128)S(1)} %get-tuple-element.126), channel_id=1, source_target_pairs={{0,8},{4,12},{8,0},{12,4},{16,24},{20,28},{24,16},{28,20},{1,9},{5... | collective-permute-start | bytes 196616 | tf_op jit(solution)/shard_map/ppermute | solution.py:128
  85.0 1.4 collective-permute-start.41
  86.3 1.3 collective-permute-start.42
  87.6 1.7 %collective-permute-start.43 = (bf16[256,128]{1,0:T(8,128)(2,1)S(1)}, bf16[256,128]{1,0:T(8,128)(2,1)S(1)}, u32[]{:S(2)}, u32[]{:S(2)}) collective-permute-start(bf16[256,128]{1,0:T(8,128)(2,1)S(1)} %get-tuple-element.108), channel_id=1, source_target_pairs={{0,3},{1,2},{2,1},{3,0},{4,7},{5,6},{6,5},{7,4},{8,11},{9,10},{10,... | collective-permute-start | bytes 196616 | tf_op jit(solution)/shard_map/ppermute | solution.py:128
  89.9 4.4 %collective-permute-done.42.refs_2_ = bf16[256,128]{1,0:T(8,128)(2,1)S(1)} collective-permute-done((bf16[256,128]{1,0:T(8,128)(2,1)S(1)}, bf16[256,128]{1,0:T(8,128)(2,1)S(1)}, u32[]{:S(2)}, u32[]{:S(2)}) %collective-permute-start.42) | collective-permute-done | bytes 65568 | tf_op jit(solution)/shard_map/ppermute | solution.py:128
  94.3 1.5 %shard_map.133 = (f32[256,128]{1,0:T(8,128)S(1)}, f32[256,128]{1,0:T(8,128)S(1)}, f32[256,128]{1,0:T(8,128)S(1)}, f32[256,128]{1,0:T(8,128)S(1)}) custom-call(bf16[1,8,512,512]{3,2,1,0:T(8,128)(2,1)S(1)} %copy-done, f32[8,256]{1,0:T(8,128)S(1)} %copy-done.1, bf16[256,128]{1,0:T(8,128)(2,1)S(1)} %get-tuple-element.105.refs_0_, ...), custom_call_target="tpu_custom_call" | custom-call | flops 1073741824 | bytes 4988928 | tf_op jit(solution)/shard_map/pallas_call | solution.py:111
  95.8 1.5 %collective-permute-start.44 = (f32[256,128]{1,0:T(8,128)S(1)}, f32[256,128]{1,0:T(8,128)S(1)}, u32[]{:S(2)}, u32[]{:S(2)}) collective-permute-start(f32[256,128]{1,0:T(8,128)S(1)} %get-tuple-element.110), channel_id=1, source_target_pairs={{0,1},{1,0},{2,3},{3,2},{4,5},{5,4},{6,7},{7,6},{8,9},{9,8},{10,11... | collective-permute-start | bytes 393224 | tf_op jit(solution)/shard_map/ppermute | solution.py:128
  97.4 0.7 collective-permute-start.45
  98.1 2.2 %collective-permute-start.46 = (f32[256,128]{1,0:T(8,128)S(1)}, f32[256,128]{1,0:T(8,128)S(1)}, u32[]{:S(2)}, u32[]{:S(2)}) collective-permute-start(f32[256,128]{1,0:T(8,128)S(1)} %get-tuple-element.112), channel_id=1, source_target_pairs={{0,3},{1,2},{2,1},{3,0},{4,7},{5,6},{6,5},{7,4},{8,11},{9,10},{10,... | collective-permute-start | bytes 393224 | tf_op jit(solution)/shard_map/ppermute | solution.py:128
  100.3 0.6 collective-permute-start.57
  100.9 6.1 %collective-permute-done.57 = f32[64,256]{1,0:T(8,128)S(1)} collective-permute-done((f32[64,256]{1,0:T(8,128)S(1)}, f32[64,256]{1,0:T(8,128)S(1)}, u32[]{:S(2)}, u32[]{:S(2)}) %collective-permute-start.57) | collective-permute-done | bytes 65568 | tf_op jit(solution)/shard_map/ppermute | solution.py:128
  107.0 2.6 %collective-permute-start.58 = (f32[64,256]{1,0:T(8,128)S(1)}, f32[64,256]{1,0:T(8,128)S(1)}, u32[]{:S(2)}, u32[]{:S(2)}) collective-permute-start(f32[64,256]{1,0:T(8,128)S(1)} %add.58), channel_id=1, source_target_pairs={{0,2},{1,3},{2,0},{3,1},{4,6},{5,7},{6,4},{7,5},{8,10},{9,11},{10,... | collective-permute-start | bytes 196616 | tf_op jit(solution)/shard_map/ppermute | solution.py:128
  110.7 3.6 %collective-permute-done.58 = f32[64,256]{1,0:T(8,128)S(1)} collective-permute-done((f32[64,256]{1,0:T(8,128)S(1)}, f32[64,256]{1,0:T(8,128)S(1)}, u32[]{:S(2)}, u32[]{:S(2)}) %collective-permute-start.58) | collective-permute-done | bytes 65568 | tf_op jit(solution)/shard_map/ppermute | solution.py:128
  114.9 3.7 %collective-permute-done.60.refs_2_ = f32[64,256]{1,0:T(8,128)S(1)} collective-permute-done((f32[64,256]{1,0:T(8,128)S(1)}, f32[64,256]{1,0:T(8,128)S(1)}, u32[]{:S(2)}, u32[]{:S(2)}) %collective-permute-start.60) | collective-permute-done | bytes 65568 | tf_op jit(solution)/shard_map/ppermute | solution.py:128
  120.7 2.4 %collective-permute-start.53 = (f32[256,128]{1,0:T(8,128)S(1)}, f32[256,128]{1,0:T(8,128)S(1)}, u32[]{:S(2)}, u32[]{:S(2)}) collective-permute-start(f32[256,128]{1,0:T(8,128)S(1)} %add.55), channel_id=1, source_target_pairs={{0,24},{4,28},{8,16},{12,20},{16,8},{20,12},{24,0},{28,4},{1,25},{... | collective-permute-start | bytes 393224 | tf_op jit(solution)/shard_map/ppermute | solution.py:128
  123.2 4.9 %shard_map.136 = (f32[256,256]{1,0:T(8,128)S(1)}, f32[1,128]{1,0:T(1,128)S(1)}) custom-call(f32[8,256]{1,0:T(8,128)S(1)} %copy-done.1, f32[64,256]{1,0:T(8,128)S(1)} %add.59.refs_0_, f32[64,256]{1,0:T(8,128)S(1)} %collective-permute-done.59.refs_1_, f32[64,256]{1,0:T(8,128)S(1)} %collective-permute-done.60.refs_2_, f32[64,256]{1,0:T(8,128)S(1)} %collective-permute-done.61.refs_3_), custom_call_target="tpu_custom_call" | custom-call | flops 6000000000 | bytes 532992 | tf_op jit(solution)/shard_map/pallas_call | solution.py:111
  128.1 4.2 %shard_map.137.refs_8_ = f32[256,256]{1,0:T(8,128)S(1)} custom-call(f32[256,256]{1,0:T(8,128)S(1)} %get-tuple-element.128.half_ref), custom_call_target="tpu_custom_call" | custom-call | flops 6000000000 | bytes 524288 | tf_op jit(solution)/shard_map/pallas_call | solution.py:111
  132.4 1.6 %collective-permute-start.32 = (f32[64,128]{1,0:T(8,128)S(1)}, f32[64,128]{1,0:T(8,128)S(1)}, u32[]{:S(2)}, u32[]{:S(2)}) collective-permute-start(f32[64,128]{1,0:T(8,128)S(1)} %get-tuple-element.101), channel_id=1, source_target_pairs={{0,2},{1,3},{2,0},{3,1},{4,6},{5,7},{6,4},{7,5},{8,10},{9,11},{10,... | collective-permute-start | bytes 98312 | tf_op jit(solution)/shard_map/ppermute | solution.py:128
  134.0 2.3 %collective-permute-start.33 = (f32[64,128]{1,0:T(8,128)S(1)}, f32[64,128]{1,0:T(8,128)S(1)}, u32[]{:S(2)}, u32[]{:S(2)}) collective-permute-start(f32[64,128]{1,0:T(8,128)S(1)} %get-tuple-element.102), channel_id=1, source_target_pairs={{0,3},{1,2},{2,1},{3,0},{4,7},{5,6},{6,5},{7,4},{8,11},{9,10},{10,... | collective-permute-start | bytes 98312 | tf_op jit(solution)/shard_map/ppermute | solution.py:128
  136.3 1.2 shard_map.138
  137.5 2.1 %collective-permute-start.63 = (f32[64,128]{1,0:T(8,128)S(1)}, f32[64,128]{1,0:T(8,128)S(1)}, u32[]{:S(2)}, u32[]{:S(2)}) collective-permute-start(f32[64,128]{1,0:T(8,128)S(1)} %get-tuple-element.131), channel_id=1, source_target_pairs={{0,2},{1,3},{2,0},{3,1},{4,6},{5,7},{6,4},{7,5},{8,10},{9,11},{10,... | collective-permute-start | bytes 98312 | tf_op jit(solution)/shard_map/ppermute | solution.py:128
  139.6 2.3 %collective-permute-start.64 = (f32[64,128]{1,0:T(8,128)S(1)}, f32[64,128]{1,0:T(8,128)S(1)}, u32[]{:S(2)}, u32[]{:S(2)}) collective-permute-start(f32[64,128]{1,0:T(8,128)S(1)} %get-tuple-element.132), channel_id=1, source_target_pairs={{0,3},{1,2},{2,1},{3,0},{4,7},{5,6},{6,5},{7,4},{8,11},{9,10},{10,... | collective-permute-start | bytes 98312 | tf_op jit(solution)/shard_map/ppermute | solution.py:128
  141.9 0.7 shard_map.131
  142.7 2.7 %collective-permute-done.64.refs_3_ = f32[64,128]{1,0:T(8,128)S(1)} collective-permute-done((f32[64,128]{1,0:T(8,128)S(1)}, f32[64,128]{1,0:T(8,128)S(1)}, u32[]{:S(2)}, u32[]{:S(2)}) %collective-permute-start.64) | collective-permute-done | bytes 32800 | tf_op jit(solution)/shard_map/ppermute | solution.py:128
  145.3 0.7 shard_map.139
  (114 shorter events, 11.3 us)
Async XLA Ops:
  2.8 14.9 %collective-permute-start.20 = (f32[256,128]{1,0:T(8,128)S(1)}, f32[256,128]{1,0:T(8,128)S(1)}, u32[]{:S(2)}, u32[]{:S(2)}) collective-permute-start(f32[256,128]{1,0:T(8,128)S(1)} %get-tuple-element.87), channel_id=1, source_target_pairs={{0,1},{1,0},{2,3},{3,2},{4,5},{5,4},{6,7},{7,6},{8,9},{9,8},{10,11... | collective-permute-start | bytes 393224 | tf_op jit(solution)/shard_map/ppermute | solution.py:128
  5.9 12.3 %collective-permute-start.21 = (f32[256,128]{1,0:T(8,128)S(1)}, f32[256,128]{1,0:T(8,128)S(1)}, u32[]{:S(2)}, u32[]{:S(2)}) collective-permute-start(f32[256,128]{1,0:T(8,128)S(1)} %get-tuple-element.88), channel_id=1, source_target_pairs={{0,2},{1,3},{2,0},{3,1},{4,6},{5,7},{6,4},{7,5},{8,10},{9,11},{10,... | collective-permute-start | bytes 393224 | tf_op jit(solution)/shard_map/ppermute | solution.py:128
  9.4 6.1 %collective-permute-start.1 = (bf16[64,512]{1,0:T(8,128)(2,1)S(1)}, bf16[64,512]{1,0:T(8,128)(2,1)S(1)}, u32[]{:S(2)}, u32[]{:S(2)}) collective-permute-start(bf16[64,512]{1,0:T(8,128)(2,1)S(1)} %bitcast_convert_fusion.refs_0_), channel_id=1, source_target_pairs={{0,8},{4,12},{8,0},{12,4},{16,24},{20,28},{24,16},{28,20},{1,9},{5... | collective-permute-start | bytes 196616 | tf_op jit(solution)/shard_map/ppermute | solution.py:128
  10.9 5.0 %collective-permute-start.3 = (bf16[64,512]{1,0:T(8,128)(2,1)S(1)}, bf16[64,512]{1,0:T(8,128)(2,1)S(1)}, u32[]{:S(2)}, u32[]{:S(2)}) collective-permute-start(bf16[64,512]{1,0:T(8,128)(2,1)S(1)} %bitcast_convert_fusion.refs_0_), channel_id=1, source_target_pairs={{0,16},{4,20},{8,24},{12,28},{16,0},{20,4},{24,8},{28,12},{1,17},{... | collective-permute-start | bytes 196616 | tf_op jit(solution)/shard_map/ppermute | solution.py:128
  12.5 5.2 %collective-permute-start.5 = (bf16[64,512]{1,0:T(8,128)(2,1)S(1)}, bf16[64,512]{1,0:T(8,128)(2,1)S(1)}, u32[]{:S(2)}, u32[]{:S(2)}) collective-permute-start(bf16[64,512]{1,0:T(8,128)(2,1)S(1)} %bitcast_convert_fusion.refs_0_), channel_id=1, source_target_pairs={{0,24},{4,28},{8,16},{12,20},{16,8},{20,12},{24,0},{28,4},{1,25},{... | collective-permute-start | bytes 196616 | tf_op jit(solution)/shard_map/ppermute | solution.py:128
  15.5 8.4 %collective-permute-start = (bf16[64,512]{1,0:T(8,128)(2,1)S(1)}, bf16[64,512]{1,0:T(8,128)(2,1)S(1)}, u32[]{:S(2)}, u32[]{:S(2)}) collective-permute-start(bf16[64,512]{1,0:T(8,128)(2,1)S(1)} %bitcast_convert_fusion.refs_0_), channel_id=1, source_target_pairs={{0,4},{4,0},{8,12},{12,8},{16,20},{20,16},{24,28},{28,24},{1,5},{5... | collective-permute-start | bytes 196616 | tf_op jit(solution)/shard_map/ppermute | solution.py:128
  15.9 7.5 %collective-permute-start.22 = (f32[256,128]{1,0:T(8,128)S(1)}, f32[256,128]{1,0:T(8,128)S(1)}, u32[]{:S(2)}, u32[]{:S(2)}) collective-permute-start(f32[256,128]{1,0:T(8,128)S(1)} %get-tuple-element.89), channel_id=1, source_target_pairs={{0,3},{1,2},{2,1},{3,0},{4,7},{5,6},{6,5},{7,4},{8,11},{9,10},{10,... | collective-permute-start | bytes 393224 | tf_op jit(solution)/shard_map/ppermute | solution.py:128
  17.6 6.3 %collective-permute-start.2 = (bf16[64,512]{1,0:T(8,128)(2,1)S(1)}, bf16[64,512]{1,0:T(8,128)(2,1)S(1)}, u32[]{:S(2)}, u32[]{:S(2)}) collective-permute-start(bf16[64,512]{1,0:T(8,128)(2,1)S(1)} %collective-permute-done.1.refs_2_), channel_id=1, source_target_pairs={{0,4},{4,0},{8,12},{12,8},{16,20},{20,16},{24,28},{28,24},{1,5},{5... | collective-permute-start | bytes 196616 | tf_op jit(solution)/shard_map/ppermute | solution.py:128
  17.6 6.3 %collective-permute-start.4 = (bf16[64,512]{1,0:T(8,128)(2,1)S(1)}, bf16[64,512]{1,0:T(8,128)(2,1)S(1)}, u32[]{:S(2)}, u32[]{:S(2)}) collective-permute-start(bf16[64,512]{1,0:T(8,128)(2,1)S(1)} %collective-permute-done.3.refs_4_), channel_id=1, source_target_pairs={{0,4},{4,0},{8,12},{12,8},{16,20},{20,16},{24,28},{28,24},{1,5},{5... | collective-permute-start | bytes 196616 | tf_op jit(solution)/shard_map/ppermute | solution.py:128
  18.1 5.8 %collective-permute-start.6 = (bf16[64,512]{1,0:T(8,128)(2,1)S(1)}, bf16[64,512]{1,0:T(8,128)(2,1)S(1)}, u32[]{:S(2)}, u32[]{:S(2)}) collective-permute-start(bf16[64,512]{1,0:T(8,128)(2,1)S(1)} %collective-permute-done.5.refs_6_), channel_id=1, source_target_pairs={{0,4},{4,0},{8,12},{12,8},{16,20},{20,16},{24,28},{28,24},{1,5},{5... | collective-permute-start | bytes 196616 | tf_op jit(solution)/shard_map/ppermute | solution.py:128
  23.8 1.4 collective-permute-start.23
  25.3 5.9 %collective-permute-start.24 = (f32[64,256]{1,0:T(8,128)S(1)}, f32[64,256]{1,0:T(8,128)S(1)}, u32[]{:S(2)}, u32[]{:S(2)}) collective-permute-start(f32[64,256]{1,0:T(8,128)S(1)} %get-tuple-element.96), channel_id=1, source_target_pairs={{0,8},{4,12},{8,0},{12,4},{16,24},{20,28},{24,16},{28,20},{1,9},{5... | collective-permute-start | bytes 196616 | tf_op jit(solution)/shard_map/ppermute | solution.py:128
  26.8 6.0 %collective-permute-start.7 = (bf16[64,512]{1,0:T(8,128)(2,1)S(1)}, bf16[64,512]{1,0:T(8,128)(2,1)S(1)}, u32[]{:S(2)}, u32[]{:S(2)}) collective-permute-start(bf16[64,512]{1,0:T(8,128)(2,1)S(1)} %get-tuple-element.71), channel_id=1, source_target_pairs={{0,1},{1,0},{2,3},{3,2},{4,5},{5,4},{6,7},{7,6},{8,9},{9,8},{10,11... | collective-permute-start | bytes 196616 | tf_op jit(solution)/shard_map/ppermute | solution.py:128
  28.2 7.9 %collective-permute-start.8 = (bf16[64,512]{1,0:T(8,128)(2,1)S(1)}, bf16[64,512]{1,0:T(8,128)(2,1)S(1)}, u32[]{:S(2)}, u32[]{:S(2)}) collective-permute-start(bf16[64,512]{1,0:T(8,128)(2,1)S(1)} %get-tuple-element.72), channel_id=1, source_target_pairs={{0,2},{1,3},{2,0},{3,1},{4,6},{5,7},{6,4},{7,5},{8,10},{9,11},{10,... | collective-permute-start | bytes 196616 | tf_op jit(solution)/shard_map/ppermute | solution.py:128
  28.2 7.9 %collective-permute-start.9 = (bf16[64,512]{1,0:T(8,128)(2,1)S(1)}, bf16[64,512]{1,0:T(8,128)(2,1)S(1)}, u32[]{:S(2)}, u32[]{:S(2)}) collective-permute-start(bf16[64,512]{1,0:T(8,128)(2,1)S(1)} %get-tuple-element.73), channel_id=1, source_target_pairs={{0,3},{1,2},{2,1},{3,0},{4,7},{5,6},{6,5},{7,4},{8,11},{9,10},{10,... | collective-permute-start | bytes 196616 | tf_op jit(solution)/shard_map/ppermute | solution.py:128
  31.2 10.9 %collective-permute-start.25 = (f32[64,256]{1,0:T(8,128)S(1)}, f32[64,256]{1,0:T(8,128)S(1)}, u32[]{:S(2)}, u32[]{:S(2)}) collective-permute-start(f32[64,256]{1,0:T(8,128)S(1)} %add.49), channel_id=1, source_target_pairs={{0,16},{4,20},{8,24},{12,28},{16,0},{20,4},{24,8},{28,12},{1,17},{... | collective-permute-start | bytes 196616 | tf_op jit(solution)/shard_map/ppermute | solution.py:128
  37.6 13.0 %collective-permute-start.10 = (f32[256,128]{1,0:T(8,128)S(1)}, f32[256,128]{1,0:T(8,128)S(1)}, u32[]{:S(2)}, u32[]{:S(2)}) collective-permute-start(f32[256,128]{1,0:T(8,128)S(1)} %get-tuple-element.75), channel_id=1, source_target_pairs={{0,1},{1,0},{2,3},{3,2},{4,5},{5,4},{6,7},{7,6},{8,9},{9,8},{10,11... | collective-permute-start | bytes 393224 | tf_op jit(solution)/shard_map/ppermute | solution.py:128
  39.1 11.7 %collective-permute-start.11 = (f32[256,128]{1,0:T(8,128)S(1)}, f32[256,128]{1,0:T(8,128)S(1)}, u32[]{:S(2)}, u32[]{:S(2)}) collective-permute-start(f32[256,128]{1,0:T(8,128)S(1)} %get-tuple-element.76), channel_id=1, source_target_pairs={{0,2},{1,3},{2,0},{3,1},{4,6},{5,7},{6,4},{7,5},{8,10},{9,11},{10,... | collective-permute-start | bytes 393224 | tf_op jit(solution)/shard_map/ppermute | solution.py:128
  39.8 11.0 %collective-permute-start.12 = (f32[256,128]{1,0:T(8,128)S(1)}, f32[256,128]{1,0:T(8,128)S(1)}, u32[]{:S(2)}, u32[]{:S(2)}) collective-permute-start(f32[256,128]{1,0:T(8,128)S(1)} %get-tuple-element.77), channel_id=1, source_target_pairs={{0,3},{1,2},{2,1},{3,0},{4,7},{5,6},{6,5},{7,4},{8,11},{9,10},{10,... | collective-permute-start | bytes 393224 | tf_op jit(solution)/shard_map/ppermute | solution.py:128
  42.1 6.4 %collective-permute-start.26 = (f32[64,256]{1,0:T(8,128)S(1)}, f32[64,256]{1,0:T(8,128)S(1)}, u32[]{:S(2)}, u32[]{:S(2)}) collective-permute-start(f32[64,256]{1,0:T(8,128)S(1)} %add.50), channel_id=1, source_target_pairs={{0,1},{1,0},{2,3},{3,2},{4,5},{5,4},{6,7},{7,6},{8,9},{9,8},{10,11... | collective-permute-start | bytes 196616 | tf_op jit(solution)/shard_map/ppermute | solution.py:128
  48.5 6.4 %collective-permute-start.27 = (f32[64,256]{1,0:T(8,128)S(1)}, f32[64,256]{1,0:T(8,128)S(1)}, u32[]{:S(2)}, u32[]{:S(2)}) collective-permute-start(f32[64,256]{1,0:T(8,128)S(1)} %add.51), channel_id=1, source_target_pairs={{0,2},{1,3},{2,0},{3,1},{4,6},{5,7},{6,4},{7,5},{8,10},{9,11},{10,... | collective-permute-start | bytes 196616 | tf_op jit(solution)/shard_map/ppermute | solution.py:128
  51.2 8.1 %collective-permute-start.14 = (f32[256,128]{1,0:T(8,128)S(1)}, f32[256,128]{1,0:T(8,128)S(1)}, u32[]{:S(2)}, u32[]{:S(2)}) collective-permute-start(f32[256,128]{1,0:T(8,128)S(1)} %get-tuple-element.81), channel_id=1, source_target_pairs={{0,4},{4,0},{8,12},{12,8},{16,20},{20,16},{24,28},{28,24},{1,5},{5... | collective-permute-start | bytes 393224 | tf_op jit(solution)/shard_map/ppermute | solution.py:128
  51.2 8.7 %collective-permute-start.16 = (f32[256,128]{1,0:T(8,128)S(1)}, f32[256,128]{1,0:T(8,128)S(1)}, u32[]{:S(2)}, u32[]{:S(2)}) collective-permute-start(f32[256,128]{1,0:T(8,128)S(1)} %get-tuple-element.83), channel_id=1, source_target_pairs={{0,4},{4,0},{8,12},{12,8},{16,20},{20,16},{24,28},{28,24},{1,5},{5... | collective-permute-start | bytes 393224 | tf_op jit(solution)/shard_map/ppermute | solution.py:128
  51.7 8.8 %collective-permute-start.18 = (f32[256,128]{1,0:T(8,128)S(1)}, f32[256,128]{1,0:T(8,128)S(1)}, u32[]{:S(2)}, u32[]{:S(2)}) collective-permute-start(f32[256,128]{1,0:T(8,128)S(1)} %get-tuple-element.85), channel_id=1, source_target_pairs={{0,4},{4,0},{8,12},{12,8},{16,20},{20,16},{24,28},{28,24},{1,5},{5... | collective-permute-start | bytes 393224 | tf_op jit(solution)/shard_map/ppermute | solution.py:128
  54.9 4.3 %collective-permute-start.29 = (f32[64,256]{1,0:T(8,128)S(1)}, f32[64,256]{1,0:T(8,128)S(1)}, u32[]{:S(2)}, u32[]{:S(2)}) collective-permute-start(f32[64,256]{1,0:T(8,128)S(1)} %add.52.refs_0_), channel_id=1, source_target_pairs={{0,8},{4,12},{8,0},{12,4},{16,24},{20,28},{24,16},{28,20},{1,9},{5... | collective-permute-start | bytes 196616 | tf_op jit(solution)/shard_map/ppermute | solution.py:128
  55.5 6.6 %collective-permute-start.28 = (f32[64,256]{1,0:T(8,128)S(1)}, f32[64,256]{1,0:T(8,128)S(1)}, u32[]{:S(2)}, u32[]{:S(2)}) collective-permute-start(f32[64,256]{1,0:T(8,128)S(1)} %add.52.refs_0_), channel_id=1, source_target_pairs={{0,4},{4,0},{8,12},{12,8},{16,20},{20,16},{24,28},{28,24},{1,5},{5... | collective-permute-start | bytes 196616 | tf_op jit(solution)/shard_map/ppermute | solution.py:128
  59.3 4.4 %collective-permute-start.30 = (f32[64,256]{1,0:T(8,128)S(1)}, f32[64,256]{1,0:T(8,128)S(1)}, u32[]{:S(2)}, u32[]{:S(2)}) collective-permute-start(f32[64,256]{1,0:T(8,128)S(1)} %collective-permute-done.29.refs_2_), channel_id=1, source_target_pairs={{0,4},{4,0},{8,12},{12,8},{16,20},{20,16},{24,28},{28,24},{1,5},{5... | collective-permute-start | bytes 196616 | tf_op jit(solution)/shard_map/ppermute | solution.py:128
  59.3 13.5 %collective-permute-start.13 = (f32[256,128]{1,0:T(8,128)S(1)}, f32[256,128]{1,0:T(8,128)S(1)}, u32[]{:S(2)}, u32[]{:S(2)}) collective-permute-start(f32[256,128]{1,0:T(8,128)S(1)} %get-tuple-element.79), channel_id=1, source_target_pairs={{0,4},{4,0},{8,12},{12,8},{16,20},{20,16},{24,28},{28,24},{1,5},{5... | collective-permute-start | bytes 393224 | tf_op jit(solution)/shard_map/ppermute | solution.py:128
  59.9 12.9 %collective-permute-start.15 = (f32[256,128]{1,0:T(8,128)S(1)}, f32[256,128]{1,0:T(8,128)S(1)}, u32[]{:S(2)}, u32[]{:S(2)}) collective-permute-start(f32[256,128]{1,0:T(8,128)S(1)} %add.45), channel_id=1, source_target_pairs={{0,8},{4,12},{8,0},{12,4},{16,24},{20,28},{24,16},{28,20},{1,9},{5... | collective-permute-start | bytes 393224 | tf_op jit(solution)/shard_map/ppermute | solution.py:128
  60.6 12.3 %collective-permute-start.17 = (f32[256,128]{1,0:T(8,128)S(1)}, f32[256,128]{1,0:T(8,128)S(1)}, u32[]{:S(2)}, u32[]{:S(2)}) collective-permute-start(f32[256,128]{1,0:T(8,128)S(1)} %add.46), channel_id=1, source_target_pairs={{0,16},{4,20},{8,24},{12,28},{16,0},{20,4},{24,8},{28,12},{1,17},{... | collective-permute-start | bytes 393224 | tf_op jit(solution)/shard_map/ppermute | solution.py:128
  62.2 10.7 %collective-permute-start.19 = (f32[256,128]{1,0:T(8,128)S(1)}, f32[256,128]{1,0:T(8,128)S(1)}, u32[]{:S(2)}, u32[]{:S(2)}) collective-permute-start(f32[256,128]{1,0:T(8,128)S(1)} %add.47), channel_id=1, source_target_pairs={{0,24},{4,28},{8,16},{12,20},{16,8},{20,12},{24,0},{28,4},{1,25},{... | collective-permute-start | bytes 393224 | tf_op jit(solution)/shard_map/ppermute | solution.py:128
  74.5 4.7 %collective-permute-start.35 = (bf16[256,128]{1,0:T(8,128)(2,1)S(1)}, bf16[256,128]{1,0:T(8,128)(2,1)S(1)}, u32[]{:S(2)}, u32[]{:S(2)}) collective-permute-start(bf16[256,128]{1,0:T(8,128)(2,1)S(1)} %get-tuple-element.104.refs_0_), channel_id=1, source_target_pairs={{0,8},{4,12},{8,0},{12,4},{16,24},{20,28},{24,16},{28,20},{1,9},{5... | collective-permute-start | bytes 196616 | tf_op jit(solution)/shard_map/ppermute | solution.py:128
  75.2 5.0 %collective-permute-start.37 = (bf16[256,128]{1,0:T(8,128)(2,1)S(1)}, bf16[256,128]{1,0:T(8,128)(2,1)S(1)}, u32[]{:S(2)}, u32[]{:S(2)}) collective-permute-start(bf16[256,128]{1,0:T(8,128)(2,1)S(1)} %get-tuple-element.104.refs_0_), channel_id=1, source_target_pairs={{0,16},{4,20},{8,24},{12,28},{16,0},{20,4},{24,8},{28,12},{1,17},{... | collective-permute-start | bytes 196616 | tf_op jit(solution)/shard_map/ppermute | solution.py:128
  76.7 5.2 %collective-permute-start.39 = (bf16[256,128]{1,0:T(8,128)(2,1)S(1)}, bf16[256,128]{1,0:T(8,128)(2,1)S(1)}, u32[]{:S(2)}, u32[]{:S(2)}) collective-permute-start(bf16[256,128]{1,0:T(8,128)(2,1)S(1)} %get-tuple-element.104.refs_0_), channel_id=1, source_target_pairs={{0,24},{4,28},{8,16},{12,20},{16,8},{20,12},{24,0},{28,4},{1,25},{... | collective-permute-start | bytes 196616 | tf_op jit(solution)/shard_map/ppermute | solution.py:128
  78.1 4.3 %collective-permute-start.34 = (bf16[256,128]{1,0:T(8,128)(2,1)S(1)}, bf16[256,128]{1,0:T(8,128)(2,1)S(1)}, u32[]{:S(2)}, u32[]{:S(2)}) collective-permute-start(bf16[256,128]{1,0:T(8,128)(2,1)S(1)} %get-tuple-element.104.refs_0_), channel_id=1, source_target_pairs={{0,4},{4,0},{8,12},{12,8},{16,20},{20,16},{24,28},{28,24},{1,5},{5... | collective-permute-start | bytes 196616 | tf_op jit(solution)/shard_map/ppermute | solution.py:128
  79.3 3.1 %collective-permute-start.36 = (bf16[256,128]{1,0:T(8,128)(2,1)S(1)}, bf16[256,128]{1,0:T(8,128)(2,1)S(1)}, u32[]{:S(2)}, u32[]{:S(2)}) collective-permute-start(bf16[256,128]{1,0:T(8,128)(2,1)S(1)} %collective-permute-done.35.refs_2_), channel_id=1, source_target_pairs={{0,4},{4,0},{8,12},{12,8},{16,20},{20,16},{24,28},{28,24},{1,5},{5... | collective-permute-start | bytes 196616 | tf_op jit(solution)/shard_map/ppermute | solution.py:128
  80.1 2.2 %collective-permute-start.38 = (bf16[256,128]{1,0:T(8,128)(2,1)S(1)}, bf16[256,128]{1,0:T(8,128)(2,1)S(1)}, u32[]{:S(2)}, u32[]{:S(2)}) collective-permute-start(bf16[256,128]{1,0:T(8,128)(2,1)S(1)} %collective-permute-done.37.refs_4_), channel_id=1, source_target_pairs={{0,4},{4,0},{8,12},{12,8},{16,20},{20,16},{24,28},{28,24},{1,5},{5... | collective-permute-start | bytes 196616 | tf_op jit(solution)/shard_map/ppermute | solution.py:128
  81.9 1.5 %collective-permute-start.54 = (f32[128,256]{1,0:T(8,128)S(1)}, f32[128,256]{1,0:T(8,128)S(1)}, u32[]{:S(2)}, u32[]{:S(2)}) collective-permute-start(f32[128,256]{1,0:T(8,128)S(1)} %get-tuple-element.124), channel_id=1, source_target_pairs={{0,4},{4,0},{8,12},{12,8},{16,20},{20,16},{24,28},{28,24},{1,5},{5... | collective-permute-start | bytes 393224 | tf_op jit(solution)/shard_map/ppermute | solution.py:128
  83.4 6.0 %collective-permute-start.55 = (f32[64,256]{1,0:T(8,128)S(1)}, f32[64,256]{1,0:T(8,128)S(1)}, u32[]{:S(2)}, u32[]{:S(2)}) collective-permute-start(f32[64,256]{1,0:T(8,128)S(1)} %get-tuple-element.126), channel_id=1, source_target_pairs={{0,8},{4,12},{8,0},{12,4},{16,24},{20,28},{24,16},{28,20},{1,9},{5... | collective-permute-start | bytes 196616 | tf_op jit(solution)/shard_map/ppermute | solution.py:128
  85.0 5.0 %collective-permute-start.41 = (bf16[256,128]{1,0:T(8,128)(2,1)S(1)}, bf16[256,128]{1,0:T(8,128)(2,1)S(1)}, u32[]{:S(2)}, u32[]{:S(2)}) collective-permute-start(bf16[256,128]{1,0:T(8,128)(2,1)S(1)} %get-tuple-element.106), channel_id=1, source_target_pairs={{0,1},{1,0},{2,3},{3,2},{4,5},{5,4},{6,7},{7,6},{8,9},{9,8},{10,11... | collective-permute-start | bytes 196616 | tf_op jit(solution)/shard_map/ppermute | solution.py:128
  86.3 8.0 %collective-permute-start.42 = (bf16[256,128]{1,0:T(8,128)(2,1)S(1)}, bf16[256,128]{1,0:T(8,128)(2,1)S(1)}, u32[]{:S(2)}, u32[]{:S(2)}) collective-permute-start(bf16[256,128]{1,0:T(8,128)(2,1)S(1)} %get-tuple-element.107), channel_id=1, source_target_pairs={{0,2},{1,3},{2,0},{3,1},{4,6},{5,7},{6,4},{7,5},{8,10},{9,11},{10,... | collective-permute-start | bytes 196616 | tf_op jit(solution)/shard_map/ppermute | solution.py:128
  87.6 6.7 %collective-permute-start.43 = (bf16[256,128]{1,0:T(8,128)(2,1)S(1)}, bf16[256,128]{1,0:T(8,128)(2,1)S(1)}, u32[]{:S(2)}, u32[]{:S(2)}) collective-permute-start(bf16[256,128]{1,0:T(8,128)(2,1)S(1)} %get-tuple-element.108), channel_id=1, source_target_pairs={{0,3},{1,2},{2,1},{3,0},{4,7},{5,6},{6,5},{7,4},{8,11},{9,10},{10,... | collective-permute-start | bytes 196616 | tf_op jit(solution)/shard_map/ppermute | solution.py:128
  89.4 10.9 %collective-permute-start.56 = (f32[64,256]{1,0:T(8,128)S(1)}, f32[64,256]{1,0:T(8,128)S(1)}, u32[]{:S(2)}, u32[]{:S(2)}) collective-permute-start(f32[64,256]{1,0:T(8,128)S(1)} %add.56), channel_id=1, source_target_pairs={{0,16},{4,20},{8,24},{12,28},{16,0},{20,4},{24,8},{28,12},{1,17},{... | collective-permute-start | bytes 196616 | tf_op jit(solution)/shard_map/ppermute | solution.py:128
  95.8 13.8 %collective-permute-start.44 = (f32[256,128]{1,0:T(8,128)S(1)}, f32[256,128]{1,0:T(8,128)S(1)}, u32[]{:S(2)}, u32[]{:S(2)}) collective-permute-start(f32[256,128]{1,0:T(8,128)S(1)} %get-tuple-element.110), channel_id=1, source_target_pairs={{0,1},{1,0},{2,3},{3,2},{4,5},{5,4},{6,7},{7,6},{8,9},{9,8},{10,11... | collective-permute-start | bytes 393224 | tf_op jit(solution)/shard_map/ppermute | solution.py:128
  97.4 12.2 %collective-permute-start.45 = (f32[256,128]{1,0:T(8,128)S(1)}, f32[256,128]{1,0:T(8,128)S(1)}, u32[]{:S(2)}, u32[]{:S(2)}) collective-permute-start(f32[256,128]{1,0:T(8,128)S(1)} %get-tuple-element.111), channel_id=1, source_target_pairs={{0,2},{1,3},{2,0},{3,1},{4,6},{5,7},{6,4},{7,5},{8,10},{9,11},{10,... | collective-permute-start | bytes 393224 | tf_op jit(solution)/shard_map/ppermute | solution.py:128
  98.1 11.5 %collective-permute-start.46 = (f32[256,128]{1,0:T(8,128)S(1)}, f32[256,128]{1,0:T(8,128)S(1)}, u32[]{:S(2)}, u32[]{:S(2)}) collective-permute-start(f32[256,128]{1,0:T(8,128)S(1)} %get-tuple-element.112), channel_id=1, source_target_pairs={{0,3},{1,2},{2,1},{3,0},{4,7},{5,6},{6,5},{7,4},{8,11},{9,10},{10,... | collective-permute-start | bytes 393224 | tf_op jit(solution)/shard_map/ppermute | solution.py:128
  100.3 6.7 %collective-permute-start.57 = (f32[64,256]{1,0:T(8,128)S(1)}, f32[64,256]{1,0:T(8,128)S(1)}, u32[]{:S(2)}, u32[]{:S(2)}) collective-permute-start(f32[64,256]{1,0:T(8,128)S(1)} %add.57), channel_id=1, source_target_pairs={{0,1},{1,0},{2,3},{3,2},{4,5},{5,4},{6,7},{7,6},{8,9},{9,8},{10,11... | collective-permute-start | bytes 196616 | tf_op jit(solution)/shard_map/ppermute | solution.py:128
  107.0 7.3 %collective-permute-start.58 = (f32[64,256]{1,0:T(8,128)S(1)}, f32[64,256]{1,0:T(8,128)S(1)}, u32[]{:S(2)}, u32[]{:S(2)}) collective-permute-start(f32[64,256]{1,0:T(8,128)S(1)} %add.58), channel_id=1, source_target_pairs={{0,2},{1,3},{2,0},{3,1},{4,6},{5,7},{6,4},{7,5},{8,10},{9,11},{10,... | collective-permute-start | bytes 196616 | tf_op jit(solution)/shard_map/ppermute | solution.py:128
  110.0 8.6 %collective-permute-start.48 = (f32[256,128]{1,0:T(8,128)S(1)}, f32[256,128]{1,0:T(8,128)S(1)}, u32[]{:S(2)}, u32[]{:S(2)}) collective-permute-start(f32[256,128]{1,0:T(8,128)S(1)} %get-tuple-element.116), channel_id=1, source_target_pairs={{0,4},{4,0},{8,12},{12,8},{16,20},{20,16},{24,28},{28,24},{1,5},{5... | collective-permute-start | bytes 393224 | tf_op jit(solution)/shard_map/ppermute | solution.py:128
  110.1 9.1 %collective-permute-start.50 = (f32[256,128]{1,0:T(8,128)S(1)}, f32[256,128]{1,0:T(8,128)S(1)}, u32[]{:S(2)}, u32[]{:S(2)}) collective-permute-start(f32[256,128]{1,0:T(8,128)S(1)} %get-tuple-element.118), channel_id=1, source_target_pairs={{0,4},{4,0},{8,12},{12,8},{16,20},{20,16},{24,28},{28,24},{1,5},{5... | collective-permute-start | bytes 393224 | tf_op jit(solution)/shard_map/ppermute | solution.py:128
  110.6 8.9 %collective-permute-start.52 = (f32[256,128]{1,0:T(8,128)S(1)}, f32[256,128]{1,0:T(8,128)S(1)}, u32[]{:S(2)}, u32[]{:S(2)}) collective-permute-start(f32[256,128]{1,0:T(8,128)S(1)} %get-tuple-element.120), channel_id=1, source_target_pairs={{0,4},{4,0},{8,12},{12,8},{16,20},{20,16},{24,28},{28,24},{1,5},{5... | collective-permute-start | bytes 393224 | tf_op jit(solution)/shard_map/ppermute | solution.py:128
  114.3 4.3 %collective-permute-start.60 = (f32[64,256]{1,0:T(8,128)S(1)}, f32[64,256]{1,0:T(8,128)S(1)}, u32[]{:S(2)}, u32[]{:S(2)}) collective-permute-start(f32[64,256]{1,0:T(8,128)S(1)} %add.59.refs_0_), channel_id=1, source_target_pairs={{0,8},{4,12},{8,0},{12,4},{16,24},{20,28},{24,16},{28,20},{1,9},{5... | collective-permute-start | bytes 196616 | tf_op jit(solution)/shard_map/ppermute | solution.py:128
  114.9 5.3 %collective-permute-start.59 = (f32[64,256]{1,0:T(8,128)S(1)}, f32[64,256]{1,0:T(8,128)S(1)}, u32[]{:S(2)}, u32[]{:S(2)}) collective-permute-start(f32[64,256]{1,0:T(8,128)S(1)} %add.59.refs_0_), channel_id=1, source_target_pairs={{0,4},{4,0},{8,12},{12,8},{16,20},{20,16},{24,28},{28,24},{1,5},{5... | collective-permute-start | bytes 196616 | tf_op jit(solution)/shard_map/ppermute | solution.py:128
  118.6 2.1 %collective-permute-start.61 = (f32[64,256]{1,0:T(8,128)S(1)}, f32[64,256]{1,0:T(8,128)S(1)}, u32[]{:S(2)}, u32[]{:S(2)}) collective-permute-start(f32[64,256]{1,0:T(8,128)S(1)} %collective-permute-done.60.refs_2_), channel_id=1, source_target_pairs={{0,4},{4,0},{8,12},{12,8},{16,20},{20,16},{24,28},{28,24},{1,5},{5... | collective-permute-start | bytes 196616 | tf_op jit(solution)/shard_map/ppermute | solution.py:128
  118.6 21.0 %collective-permute-start.31 = (f32[64,128]{1,0:T(8,128)S(1)}, f32[64,128]{1,0:T(8,128)S(1)}, u32[]{:S(2)}, u32[]{:S(2)}) collective-permute-start(f32[64,128]{1,0:T(8,128)S(1)} %get-tuple-element.100), channel_id=1, source_target_pairs={{0,1},{1,0},{2,3},{3,2},{4,5},{5,4},{6,7},{7,6},{8,9},{9,8},{10,11... | collective-permute-start | bytes 98312 | tf_op jit(solution)/shard_map/ppermute | solution.py:128
  119.2 13.2 %collective-permute-start.47 = (f32[256,128]{1,0:T(8,128)S(1)}, f32[256,128]{1,0:T(8,128)S(1)}, u32[]{:S(2)}, u32[]{:S(2)}) collective-permute-start(f32[256,128]{1,0:T(8,128)S(1)} %get-tuple-element.114), channel_id=1, source_target_pairs={{0,4},{4,0},{8,12},{12,8},{16,20},{20,16},{24,28},{28,24},{1,5},{5... | collective-permute-start | bytes 393224 | tf_op jit(solution)/shard_map/ppermute | solution.py:128
  119.5 14.5 %collective-permute-start.49 = (f32[256,128]{1,0:T(8,128)S(1)}, f32[256,128]{1,0:T(8,128)S(1)}, u32[]{:S(2)}, u32[]{:S(2)}) collective-permute-start(f32[256,128]{1,0:T(8,128)S(1)} %add.53), channel_id=1, source_target_pairs={{0,8},{4,12},{8,0},{12,4},{16,24},{20,28},{24,16},{28,20},{1,9},{5... | collective-permute-start | bytes 393224 | tf_op jit(solution)/shard_map/ppermute | solution.py:128
  120.2 16.1 %collective-permute-start.51 = (f32[256,128]{1,0:T(8,128)S(1)}, f32[256,128]{1,0:T(8,128)S(1)}, u32[]{:S(2)}, u32[]{:S(2)}) collective-permute-start(f32[256,128]{1,0:T(8,128)S(1)} %add.54), channel_id=1, source_target_pairs={{0,16},{4,20},{8,24},{12,28},{16,0},{20,4},{24,8},{28,12},{1,17},{... | collective-permute-start | bytes 393224 | tf_op jit(solution)/shard_map/ppermute | solution.py:128
  120.7 15.5 %collective-permute-start.53 = (f32[256,128]{1,0:T(8,128)S(1)}, f32[256,128]{1,0:T(8,128)S(1)}, u32[]{:S(2)}, u32[]{:S(2)}) collective-permute-start(f32[256,128]{1,0:T(8,128)S(1)} %add.55), channel_id=1, source_target_pairs={{0,24},{4,28},{8,16},{12,20},{16,8},{20,12},{24,0},{28,4},{1,25},{... | collective-permute-start | bytes 393224 | tf_op jit(solution)/shard_map/ppermute | solution.py:128
  132.4 9.5 %collective-permute-start.32 = (f32[64,128]{1,0:T(8,128)S(1)}, f32[64,128]{1,0:T(8,128)S(1)}, u32[]{:S(2)}, u32[]{:S(2)}) collective-permute-start(f32[64,128]{1,0:T(8,128)S(1)} %get-tuple-element.101), channel_id=1, source_target_pairs={{0,2},{1,3},{2,0},{3,1},{4,6},{5,7},{6,4},{7,5},{8,10},{9,11},{10,... | collective-permute-start | bytes 98312 | tf_op jit(solution)/shard_map/ppermute | solution.py:128
  134.0 7.9 %collective-permute-start.33 = (f32[64,128]{1,0:T(8,128)S(1)}, f32[64,128]{1,0:T(8,128)S(1)}, u32[]{:S(2)}, u32[]{:S(2)}) collective-permute-start(f32[64,128]{1,0:T(8,128)S(1)} %get-tuple-element.102), channel_id=1, source_target_pairs={{0,3},{1,2},{2,1},{3,0},{4,7},{5,6},{6,5},{7,4},{8,11},{9,10},{10,... | collective-permute-start | bytes 98312 | tf_op jit(solution)/shard_map/ppermute | solution.py:128
  137.4 5.2 %collective-permute-start.62 = (f32[64,128]{1,0:T(8,128)S(1)}, f32[64,128]{1,0:T(8,128)S(1)}, u32[]{:S(2)}, u32[]{:S(2)}) collective-permute-start(f32[64,128]{1,0:T(8,128)S(1)} %get-tuple-element.130), channel_id=1, source_target_pairs={{0,1},{1,0},{2,3},{3,2},{4,5},{5,4},{6,7},{7,6},{8,9},{9,8},{10,11... | collective-permute-start | bytes 98312 | tf_op jit(solution)/shard_map/ppermute | solution.py:128
  137.5 5.1 %collective-permute-start.63 = (f32[64,128]{1,0:T(8,128)S(1)}, f32[64,128]{1,0:T(8,128)S(1)}, u32[]{:S(2)}, u32[]{:S(2)}) collective-permute-start(f32[64,128]{1,0:T(8,128)S(1)} %get-tuple-element.131), channel_id=1, source_target_pairs={{0,2},{1,3},{2,0},{3,1},{4,6},{5,7},{6,4},{7,5},{8,10},{9,11},{10,... | collective-permute-start | bytes 98312 | tf_op jit(solution)/shard_map/ppermute | solution.py:128
  139.6 5.7 %collective-permute-start.64 = (f32[64,128]{1,0:T(8,128)S(1)}, f32[64,128]{1,0:T(8,128)S(1)}, u32[]{:S(2)}, u32[]{:S(2)}) collective-permute-start(f32[64,128]{1,0:T(8,128)S(1)} %get-tuple-element.132), channel_id=1, source_target_pairs={{0,3},{1,2},{2,1},{3,0},{4,7},{5,6},{6,5},{7,4},{8,11},{9,10},{10,... | collective-permute-start | bytes 98312 | tf_op jit(solution)/shard_map/ppermute | solution.py:128
  (6 other events, 27.5 us)
